TPU v7x, 768 devices: a whole 4x8x12 slice. The times are simulated.
768 devices in a mesh: dp: 64 (over z_lo, y, core), chan: 12 (over x, z_hi).
Axes of the slice: x: 4, y: 8, z: 12 (z_hi: 3, z_lo: 4; z = z_hi * 4 + z_lo), core: 2. Of those that a mesh axis runs over, the one named last changes fastest.
Arguments:
- pixels: bfloat16 [6144, 1536], P('dp', 'chan'), may hold values from -6 to 6
- embed_weight: bfloat16 [96, 16, 1024], P('chan'), may hold values from -1.5 to 1.5
- channel_bias: bfloat16 [96, 1024], P('chan'), may hold values from -3 to 3
- agg_query: bfloat16 [12, 1024], P('chan'), may hold values from -0.375 to 0.375
- key_weight: bfloat16 [1024, 768], P(None, 'chan'), may hold values from -0.1875 to 0.1875
- value_weight: bfloat16 [1024, 768], P(None, 'chan'), may hold values from -0.1875 to 0.1875
- final_query: bfloat16 [12, 64], P('chan'), may hold values from -10 to 10
- out_weight: bfloat16 [768, 1024], P('chan'), may hold values from -0.21875 to 0.21875
- group_counts: int32 [12], P('chan'), may hold values from 4 to 8, as said below
- grad_output: bfloat16 [6144, 1024], P('dp'), may hold values from -0.078125 to 0.078125
Outputs:
- layer_out: bfloat16 [6144, 1024], P('dp')
- grad_embed: float32 [96, 16, 1024], P('chan')
- grad_bias: float32 [96, 1024], P('chan')
- grad_agg: float32 [12, 1024], P('chan')
- grad_key: float32 [1024, 768], P(None, 'chan')
- grad_value: float32 [1024, 768], P(None, 'chan')
- grad_query: float32 [12, 64], P('chan')
- grad_out: float32 [768, 1024], P('chan')
Inputs may be any that keep to these rules, and one draw needn't show every extreme that they name: A group's first group_counts[g] channels are live; some group has all 8 live.
All inputs are finite; a program needn't handle non-finite values.
Results may differ from a plain program's by a relative error of at most 0.018.
The roundings to bfloat16 on the way count: a program that leaves them out, or rounds other values in their place, can miss the bound.
Values may be sent and summed in bfloat16 or wider, within the bound.
A program may use at most 32 MiB of HBM per device.

v0:
```python
import math

import jax
import jax.numpy as jnp
from jax import lax
from jax.sharding import Mesh
from jax.sharding import PartitionSpec as P

CHAN = ("chan_0", "chan_1")


softcap = 15.0


def in_blocks(shard, dim, devices):
    before, after = (shard.shape[:dim], shard.shape[dim + 1 :])
    return jnp.moveaxis(shard.reshape(*before, devices, -1, *after), dim, 0)


def summed_on_arrival(shard, axis, dim):
    devices = lax.axis_size(axis)
    blocks = lax.all_to_all(in_blocks(shard, dim, devices), axis, 0, 0, tiled=True)
    return jnp.sum(blocks.astype(jnp.float32), axis=0)


def laid_out(blocks, dim):
    blocks = jnp.moveaxis(blocks, 0, dim)
    lengths = blocks.shape
    return blocks.reshape(*lengths[:dim], lengths[dim] * lengths[dim + 1], *lengths[dim + 2 :])


def from_everyone(shard, axis):
    devices = lax.axis_size(axis)
    return lax.all_to_all(
        jnp.broadcast_to(shard[None], (devices, *shard.shape)), axis, 0, 0, tiled=True
    )


def collect(shard, axis, dim):
    return laid_out(from_everyone(shard, axis), dim)


def sum_by_axis(shard, axes, dim):
    for axis in axes:
        shard = lax.psum_scatter(shard, axis, scatter_dimension=dim, tiled=True)
    return shard


def per_device(
    pixels,
    embed_weight,
    channel_bias,
    agg_query,
    key_weight,
    value_weight,
    final_query,
    out_weight,
    group_counts,
    grad_output,
):
    tok_rows = pixels.shape[0]
    channel_count = embed_weight.shape[0]
    pixel_count = embed_weight.shape[1]
    head_size = key_weight.shape[1]
    patches = pixels.reshape(tok_rows, channel_count, pixel_count)
    embedded = (
        jnp.einsum("tcp,cpd->tcd", patches, embed_weight, preferred_element_type=jnp.float32)
        + channel_bias.astype(jnp.float32)[None]
    ).astype(jnp.bfloat16)
    live_mask = (jnp.arange(channel_count, dtype=jnp.int32) < group_counts[0]).astype(jnp.float32)
    query_row = agg_query[0]
    agg_capped = softcap * jnp.tanh(
        jnp.einsum("tcd,d->tc", embedded, query_row, preferred_element_type=jnp.float32) / softcap
    )
    agg_exp = jnp.exp(agg_capped) * live_mask[None]
    agg_weight = agg_exp / jnp.sum(agg_exp, -1, keepdims=True)
    agg_round = agg_weight.astype(jnp.bfloat16)
    group_token = jnp.einsum(
        "tc,tcd->td", agg_round, embedded, preferred_element_type=jnp.float32
    ).astype(jnp.bfloat16)
    gathered = lax.all_gather(group_token[:, None, :], CHAN, axis=1, tiled=True)
    proj_weight = jnp.concatenate([key_weight, value_weight], axis=1)
    key_value = jnp.einsum(
        "tgd,de->tge", gathered, proj_weight, preferred_element_type=jnp.float32
    ).astype(jnp.bfloat16)
    keys_part = key_value[:, :, :head_size]
    values_part = key_value[:, :, head_size:]
    query_head = final_query[0]
    head_capped = softcap * jnp.tanh(
        jnp.einsum("tgk,k->tg", keys_part, query_head, preferred_element_type=jnp.float32)
        / math.sqrt(head_size)
        / softcap
    )
    head_exp = jnp.exp(head_capped)
    head_prob = head_exp / jnp.sum(head_exp, -1, keepdims=True)
    head_round = head_prob.astype(jnp.bfloat16)
    attended = jnp.einsum(
        "tg,tgk->tk", head_round, values_part, preferred_element_type=jnp.float32
    ).astype(jnp.bfloat16)
    partial_out = jnp.dot(attended, out_weight, preferred_element_type=jnp.float32)
    share_rows = summed_on_arrival(partial_out.astype(jnp.bfloat16), CHAN, 0).astype(jnp.bfloat16)
    layer_out = collect(share_rows, CHAN, 0)
    grad_out = lax.dot_general(
        attended, grad_output, (((0,), (0,)), ((), ())), preferred_element_type=jnp.float32
    )
    attended_grad = lax.dot_general(
        grad_output, out_weight, (((1,), (1,)), ((), ())), preferred_element_type=jnp.float32
    ).astype(jnp.bfloat16)
    prob_grad = jnp.einsum(
        "tk,tgk->tg", attended_grad, values_part, preferred_element_type=jnp.float32
    )
    value_grad = (
        head_round.astype(jnp.float32)[:, :, None] * attended_grad.astype(jnp.float32)[:, None, :]
    ).astype(jnp.bfloat16)
    score_grad = head_prob * (prob_grad - jnp.sum(head_prob * prob_grad, -1, keepdims=True))
    raw_grad = score_grad * (1.0 - (head_capped / softcap) ** 2) / math.sqrt(head_size)
    key_grad = (raw_grad[:, :, None] * query_head.astype(jnp.float32)[None, None, :]).astype(
        jnp.bfloat16
    )
    grad_query = jnp.einsum("tg,tgk->k", raw_grad, keys_part.astype(jnp.float32))
    both_grad = jnp.concatenate([key_grad, value_grad], axis=2)
    grad_both = jnp.einsum("tgd,tge->de", gathered, both_grad, preferred_element_type=jnp.float32)
    grad_key = grad_both[:, :head_size]
    grad_value = grad_both[:, head_size:]
    head_part = jnp.einsum(
        "tge,de->tgd", both_grad, proj_weight, preferred_element_type=jnp.float32
    ).astype(jnp.bfloat16)
    token_grad = sum_by_axis(head_part, CHAN, 1).astype(jnp.float32)[:, 0, :]
    mix_grad = jnp.einsum("td,tcd->tc", token_grad, embedded.astype(jnp.float32))
    mix_weighted = jnp.sum(agg_weight * mix_grad, -1, keepdims=True)
    agg_raw_grad = agg_weight * (mix_grad - mix_weighted) * (1.0 - (agg_capped / softcap) ** 2)
    embed_grad = (
        agg_round.astype(jnp.float32)[:, :, None] * token_grad[:, None, :]
        + agg_raw_grad[:, :, None] * query_row.astype(jnp.float32)[None, None, :]
    ).astype(jnp.bfloat16)
    grad_agg = jnp.einsum("tc,tcd->d", agg_raw_grad, embedded.astype(jnp.float32))[None]
    grad_embed = jnp.einsum("tcp,tcd->cpd", patches, embed_grad, preferred_element_type=jnp.float32)
    grad_bias = jnp.sum(embed_grad.astype(jnp.float32), 0)
    summed = lax.psum(
        (grad_embed, grad_bias, grad_agg, grad_key, grad_value, grad_query[None], grad_out), "dp"
    )
    return (layer_out, summed[0], summed[1], summed[2], summed[3], summed[4], summed[5], summed[6])


def solution(mesh):
    finer = Mesh(mesh.devices.reshape(mesh.shape["dp"], 4, 3), ("dp", "chan_0", "chan_1"))
    in_specs = (
        P("dp", CHAN),
        P(CHAN, None, None),
        P(CHAN, None),
        P(CHAN, None),
        P(None, CHAN),
        P(None, CHAN),
        P(CHAN, None),
        P(CHAN, None),
        P(CHAN),
        P("dp", None),
    )
    out_specs = (
        P("dp", None),
        P(CHAN, None, None),
        P(CHAN, None),
        P(CHAN, None),
        P(None, CHAN),
        P(None, CHAN),
        P(CHAN, None),
        P(CHAN, None),
    )
    return jax.shard_map(
        per_device, mesh=finer, in_specs=in_specs, out_specs=out_specs, check_vma=False
    )
```

profile of v0, /device:TPU:1, one launch (start us, length us, event | category | flops | bytes accessed | tf_op | source)
XLA Modules:
  0.0 759.9 jit_solution(13148794151216111867)
XLA Ops:
  7.9 0.8 copy.23
  10.2 1.3 fusion.38
  12.3 1.1 fusion.14
  13.4 0.7 copy.70
  15.4 97.1 %all-gather.3.cloned.1.call-done = bf16[96,12288]{1,0:T(8,128)(2,1)} async-done(((bf16[96,1024]{1,0:T(8,128)(2,1)}), bf16[96,12288]{1,0:T(8,128)(2,1)}) %all-gather.3.cloned.1.call-update) | async-done | bytes 2359312 | tf_op jit(solution)/shard_map/all_gather | solution.py:81
  112.5 2.5 fusion.20
  116.0 1.0 multiply_convert_fusion
  117.1 2.3 convolution_convert_fusion
  119.4 44.9 %reduce-scatter.3.cloned.1.call-done = bf16[96,3,1024]{2,0,1:T(8,128)(2,1)} async-done(((bf16[96,12,1024]{2,0,1:T(8,128)(2,1)}), bf16[96,3,1024]{2,0,1:T(8,128)(2,1)}) %reduce-scatter.3.cloned.1.call-update) | async-done | bytes 589840 | tf_op jit(solution)/shard_map/reduce_scatter | solution.py:45
  165.0 0.9 fusion.23
  165.8 8.8 %all-to-all-start = ((bf16[12,8,1024]{2,1,0:T(8,128)(2,1)}), bf16[12,8,1024]{2,1,0:T(8,128)(2,1)S(1)}, u32[]{:S(2)}, u32[]{:S(2)}) async-start(bf16[12,8,1024]{2,1,0:T(8,128)(2,1)} %fusion.23), calls=%async_computation | async-start | bytes 393216 | tf_op jit(solution)/shard_map/all_to_all | solution.py:22
  174.7 0.9 fusion.31
  175.6 2.3 fusion.17
  177.9 0.8 fusion.49
  178.7 31.1 %reduce-scatter.5.cloned.1.call-done = bf16[96,1,1024]{2,0,1:T(8,128)(2,1)} async-done(((bf16[96,3,1024]{2,0,1:T(8,128)(2,1)}), bf16[96,1,1024]{2,0,1:T(8,128)(2,1)}) %reduce-scatter.5.cloned.1.call-update) | async-done | bytes 196624 | tf_op jit(solution)/shard_map/reduce_scatter | solution.py:45
  209.8 2.2 fusion.12
  212.4 1.4 fusion.16
  214.5 5.4 all-to-all-start.1
  220.1 11.5 %all-to-all-done.1 = bf16[12,8,1024]{2,1,0:T(8,128)(2,1)S(1)} async-done(((bf16[12,8,1024]{2,1,0:T(8,128)(2,1)}), bf16[12,8,1024]{2,1,0:T(8,128)(2,1)S(1)}, u32[]{:S(2)}, u32[]{:S(2)}) %all-to-all-start.1) | async-done | bytes 196640 | tf_op jit(solution)/shard_map/all_to_all | solution.py:34
  232.5 265.1 %all-reduce = (f32[8,1024]{1,0:T(8,128)}, f32[1,1024]{1,0:T(1,128)}, f32[1,64]{1,0:T(1,128)}) all-reduce(f32[8,1024]{1,0:T(8,128)S(1)} %convert_reduce_fusion, f32[1,1024]{1,0:T(1,128)S(1)} %convolution_bitcast_fusion, f32[1,64]{1,0:T(1,128)S(1)} %convolution_bitcast_fusion.1), channel_id=1, replica_groups=mesh['dp'=64,'chan_0'=4,'chan_1'=3] {'dp'}, use_global_device_ids=true, to_apply=%region_9.0 | all-reduce | flops 9280 | bytes 74240 | tf_op jit(solution)/shard_map/psum | solution.py:139
  497.6 249.1 %all-reduce.4.cloned.1.call-done = (f32[8,16,1024]{2,1,0:T(8,128)}, f32[1024,64]{0,1:T(8,128)}, f32[1024,64]{0,1:T(8,128)}, f32[64,1024]{1,0:T(8,128)}) async-done(((f32[8,16,1024]{2,1,0:T(8,128)}, f32[1024,64]{0,1:T(8,128)}, f32[1024,64]{0,1:T(8,128)}, f32[64,1024]{1,0:T(8,128)}), (f32[8,16,1024]{2,1,0:T(8,128)}, f32[1024,64]{0,1:T(8,128)}, f32[1024,64]{0,1:T(8,128)}, ...) | async-done | bytes 1310736 | tf_op jit(solution)/shard_map/psum | solution.py:139
  747.4 1.9 copy.78
  749.3 1.7 copy.79
  751.0 1.7 copy.80
  (70 shorter events, 8.6 us)
Async XLA Ops:
  7.2 2.3 copy-start
  7.2 105.3 %all-gather.3.cloned.1.call-start = ((), (), s32[]{:S(2)}) async-start(), calls=%async_computation.6 | async-start | bytes 2555904 | tf_op jit(solution)/shard_map/all_gather | solution.py:81
  7.9 3.7 copy-start.9
  10.1 4.1 copy-start.1
  10.1 4.1 copy-start.2
  10.1 4.4 copy-start.6
  10.2 4.6 copy-start.7
  11.5 3.4 copy-start.13
  11.6 0.5 copy-start.11
  14.2 150.2 %reduce-scatter.3.cloned.1.call-start = ((), (), s32[]{:S(2)}) async-start(), calls=%async_computation.4 | async-start | bytes 2949120 | tf_op jit(solution)/shard_map/reduce_scatter | solution.py:45
  117.1 47.3 %copy-start.8 = (bf16[1,1024]{1,0:T(2,128)(2,1)S(1)}, bf16[1,1024]{1,0:T(2,128)(2,1)}, u32[]{:S(2)}) copy-start(bf16[1,1024]{1,0:T(2,128)(2,1)} %param.13) | copy-start | bytes 6148
  119.4 45.6 %copy-start.3 = (bf16[64,1024]{1,0:T(8,128)(2,1)S(1)}, bf16[64,1024]{1,0:T(8,128)(2,1)}, u32[]{:S(2)}) copy-start(bf16[64,1024]{1,0:T(8,128)(2,1)} %param.17) | copy-start | bytes 393220
  119.4 90.4 %reduce-scatter.5.cloned.1.call-start = ((), (), s32[]{:S(2)}) async-start(), calls=%async_computation.5 | async-start | bytes 786432 | tf_op jit(solution)/shard_map/reduce_scatter | solution.py:45
  165.8 47.9 %all-to-all-start = ((bf16[12,8,1024]{2,1,0:T(8,128)(2,1)}), bf16[12,8,1024]{2,1,0:T(8,128)(2,1)S(1)}, u32[]{:S(2)}, u32[]{:S(2)}) async-start(bf16[12,8,1024]{2,1,0:T(8,128)(2,1)} %fusion.23), calls=%async_computation | async-start | bytes 393216 | tf_op jit(solution)/shard_map/all_to_all | solution.py:22
  174.6 572.1 %all-reduce.4.cloned.1.call-start = ((), (), s32[]{:S(2)}) async-start(), calls=%async_computation.7 | async-start | bytes 2621440 | tf_op jit(solution)/shard_map/psum | solution.py:139
  178.7 33.4 %copy-start.10 = (f32[8]{0:T(128)S(1)}, f32[8]{0:T(128)}, u32[]{:S(2)}) copy-start(f32[8]{0:T(128)} %copy-done.9) | copy-start | bytes 100
  178.7 33.4 %copy-start.12 = (f32[96]{0:T(128)S(1)}, f32[96]{0:T(128)}, u32[]{:S(2)}) copy-start(f32[96]{0:T(128)} %copy-done.11) | copy-start | bytes 1156
  209.8 2.5 copy-start.5
  214.5 17.1 %all-to-all-start.1 = ((bf16[12,8,1024]{2,1,0:T(8,128)(2,1)}), bf16[12,8,1024]{2,1,0:T(8,128)(2,1)S(1)}, u32[]{:S(2)}, u32[]{:S(2)}) async-start(bf16[12,8,1024]{2,1,0:T(8,128)(2,1)} %broadcast_in_dim.9), calls=%async_computation.1 | async-start | bytes 393216 | tf_op jit(solution)/shard_map/all_to_all | solution.py:34
  746.7 5.9 copy-start.4
Sparse Core Ops, SparseCore 0:
  14.3 98.1 all-gather.2
  119.5 44.8 reduce-scatter.2
  167.5 42.2 reduce-scatter.4
  213.9 532.8 all-reduce.3
where the time goes:
time: 761 us; the launch traced here: 760 us
  waiting for transfers between devices  434 us (57%)
  blocking collectives  265 us (35%)
  matrix products  16.7 us (2%)
  between operations  14.7 us (2%)
  starting transfers between devices  14.3 us (2%)
  local copies, waits for them, and re-layouts  11.4 us (1%)
    psum x1, blocking collectives, per_device(): lax.psum((grad_embed, grad_bias, grad_agg, grad_key, grad_value, grad_que...  265 us
    psum x1, waiting for transfers between devices, per_device(): lax.psum((grad_embed, grad_bias, grad_agg, grad_key, grad_value, grad_que...  249 us
    all_gather x1, waiting for transfers between devices, per_device(): gathered = lax.all_gather(group_token[:, None, :], CHAN, axis=1, tiled=True)  97.1 us
    reduce_scatter x2, waiting for transfers between devices, sum_by_axis(): shard = lax.psum_scatter(shard, axis, scatter_dimension=dim, tiled=True)  76 us
  transfers between devices with their start and end apart: 6, of which 5 were waited for; matrix products, arithmetic and copies ran while one was open for 2% of the time, Pallas kernels for 0%

commit v1 on v0

v1 whole, which is shorter than its diff:
```python
import jax
import jax.numpy as jnp
from jax import lax
from jax.experimental import pallas as pl
from jax.experimental.pallas import tpu as pltpu
from jax.sharding import PartitionSpec as P

MESH = pl.DeviceIdType.MESH
NX, NH, NY, NL = 4, 3, 8, 4
CH = NX * NH
TOK, D = 96, 1024
HEADS, HD = 12, 64
PARTS = 3
PR = TOK // PARTS
PH = PR // 2
CAP = 15.0
LANES = 640

f32, bf16 = jnp.float32, jnp.bfloat16


def coords():
    dp, ch = lax.axis_index("dp"), lax.axis_index("chan")
    return dp, ch


def gather_kernel(tok, wp, kt, tok_all, w_all, kt_all, loc, sz, rz, sx, rx, sw, rw, sy, ry, sb, rb):
    dp, ch = coords()
    x, zh = ch // NH, ch % NH
    core, y, zl = dp % 2, (dp // 2) % NY, dp // (2 * NY)
    xn, xp = (x + 1) % NX, (x + NX - 1) % NX
    yn, yp = (y + 1) % NY, (y + NY - 1) % NY

    def at_chan(x_, z_):
        return (dp, x_ * NH + z_)

    def at_dp(y_, c_):
        return (zl * (2 * NY) + y_ * 2 + c_, ch)

    zdev = [at_chan(x, (zh + k + 1) % NH) for k in range(2)]
    xdev = [at_chan(xn, zh), at_chan(xp, zh)]
    ydev = [at_dp(yn, core), at_dp(yp, core)]
    sib = at_dp(y, 1 - core)

    barrier = pltpu.get_barrier_semaphore()
    for dev in zdev + xdev + ydev + [sib]:
        pl.semaphore_signal(barrier, inc=1, device_id=dev, device_id_type=MESH)
    pl.semaphore_wait(barrier, 7)

    started = []

    def send(src, dst, ss, rs, dev):
        copy = pltpu.make_async_remote_copy(
            src_ref=src, dst_ref=dst, send_sem=ss, recv_sem=rs, device_id=dev, device_id_type=MESH
        )
        copy.start()
        started.append(copy)

    def arrive(dst, ss, rs):
        pltpu.make_async_remote_copy(
            src_ref=dst, dst_ref=dst, send_sem=ss, recv_sem=rs, device_id=sib, device_id_type=MESH
        ).wait_recv()

    def owner(dx, k):
        return ((x + NX - dx) % NX) * NH + (zh + NH - k) % NH

    blk = y * 2 + core
    small = [(wp, lambda c: w_all.at[blk, c]), (kt, lambda c: kt_all.at[c])]

    def part(c, p):
        return tok_all.at[c, pl.ds(p * PR, PR)]

    def half(c, p, h):
        return tok_all.at[c, pl.ds(p * PR + h * PH, PH)]

    local = [
        pltpu.make_async_copy(tok, tok_all.at[ch], loc.at[0]),
        pltpu.make_async_copy(wp, w_all.at[blk, ch], loc.at[1]),
        pltpu.make_async_copy(kt, kt_all.at[ch], loc.at[2]),
    ]
    for copy in local:
        copy.start()
    for i, (src, dst) in enumerate(small):
        for k in range(2):
            send(src, dst(ch), sw.at[i, k], rw.at[i, k], zdev[k])
        for d in range(2):
            send(src, dst(ch), sw.at[i, 2 + 3 * d], rw.at[i, 2 + 3 * d], xdev[d])
    for p in range(PARTS):
        mine = tok.at[pl.ds(p * PR, PR)]
        for k in range(2):
            send(mine, part(ch, p), sz.at[k, p], rz.at[k, p], zdev[k])
        for d in range(2):
            send(mine, part(ch, p), sx.at[d, 0, p], rx.at[d, 0, p], xdev[d])
    for copy in local:
        copy.wait()

    for k in (1, 2):
        for i, (_, dst) in enumerate(small):
            c = owner(0, k)
            arrive(dst(c), sw.at[i, k - 1], rw.at[i, k - 1])
            for d in range(2):
                send(dst(c), dst(c), sw.at[i, 2 + 3 * d + k], rw.at[i, 2 + 3 * d + k], xdev[d])
    for k in range(3):
        for i, (_, dst) in enumerate(small):
            c = owner(1, k)
            arrive(dst(c), sw.at[i, 2 + k], rw.at[i, 2 + k])
            send(dst(c), dst(c), sw.at[i, 8 + k], rw.at[i, 8 + k], xdev[0])

    def relay(k, p):
        c = owner(1, k)
        arrive(part(c, p), sx.at[0, k, p], rx.at[0, k, p])
        send(half(c, p, 0), half(c, p, 0), sx.at[2, k, p], rx.at[2, k, p], xdev[0])
        c = owner(NX - 1, k)
        arrive(part(c, p), sx.at[1, k, p], rx.at[1, k, p])
        send(half(c, p, 1), half(c, p, 1), sx.at[3, k, p], rx.at[3, k, p], xdev[1])

    for p in range(PARTS):
        relay(0, p)
    for k in range(3):
        for i, (_, dst) in enumerate(small):
            c = owner(NX - 1, k)
            arrive(dst(c), sw.at[i, 5 + k], rw.at[i, 5 + k])
            c = owner(2, k)
            arrive(dst(c), sw.at[i, 8 + k], rw.at[i, 8 + k])

    def sub(y_, h):
        return w_all.at[((y_ + 2 * NY) % NY) * 2 + core, pl.ds(6 * h, 6)]

    def ystep(s):
        for h in range(2):
            if s < 3 or h == 0:
                send(sub(y - s, h), sub(y - s, h), sy.at[0, s, h], ry.at[0, s, h], ydev[0])
            if s < 3 or h == 1:
                send(sub(y + s, h), sub(y + s, h), sy.at[1, s, h], ry.at[1, s, h], ydev[1])

    def yarrive(s):
        for h in range(2):
            if s < 3 or h == 0:
                arrive(sub(y - 1 - s, h), sy.at[0, s, h], ry.at[0, s, h])
                send(sub(y - 1 - s, h), sub(y - 1 - s, h), sb.at[0, s, h], rb.at[0, s, h], sib)
            if s < 3 or h == 1:
                arrive(sub(y + 1 + s, h), sy.at[1, s, h], ry.at[1, s, h])
                send(sub(y + 1 + s, h), sub(y + 1 + s, h), sb.at[1, s, h], rb.at[1, s, h], sib)
            if s + 1 < 3 or (s + 1 == 3 and h == 0):
                send(sub(y - 1 - s, h), sub(y - 1 - s, h), sy.at[0, s + 1, h], ry.at[0, s + 1, h], ydev[0])
            if s + 1 < 3 or (s + 1 == 3 and h == 1):
                send(sub(y + 1 + s, h), sub(y + 1 + s, h), sy.at[1, s + 1, h], ry.at[1, s + 1, h], ydev[1])

    ystep(0)
    for h in range(2):
        send(sub(y, h), sub(y, h), sb.at[2, 0, h], rb.at[2, 0, h], sib)
    for p in range(PARTS):
        for k in (1, 2):
            c = owner(0, k)
            arrive(part(c, p), sz.at[k - 1, p], rz.at[k - 1, p])
            for d in range(2):
                send(part(c, p), part(c, p), sx.at[d, k, p], rx.at[d, k, p], xdev[d])
        yarrive(p)
        for k in (1, 2):
            relay(k, p)
    yarrive(3)
    for k in range(3):
        for p in range(PARTS):
            c = owner(2, k)
            arrive(half(c, p, 0), sx.at[2, k, p], rx.at[2, k, p])
            arrive(half(c, p, 1), sx.at[3, k, p], rx.at[3, k, p])

    def theirs(y_, h):
        return w_all.at[((y_ + 2 * NY) % NY) * 2 + 1 - core, pl.ds(6 * h, 6)]

    for h in range(2):
        arrive(theirs(y, h), sb.at[2, 0, h], rb.at[2, 0, h])
        for s in range(4):
            if s < 3 or h == 0:
                arrive(theirs(y - 1 - s, h), sb.at[0, s, h], rb.at[0, s, h])
            if s < 3 or h == 1:
                arrive(theirs(y + 1 + s, h), sb.at[1, s, h], rb.at[1, s, h])
    for copy in started:
        copy.wait_send()


def gather_all(tok, wp, kt):
    any_ = pl.BlockSpec(memory_space=pl.ANY)
    vmem = pl.BlockSpec(memory_space=pltpu.VMEM)
    dma = pltpu.SemaphoreType.DMA
    return pl.pallas_call(
        gather_kernel,
        out_shape=(
            jax.ShapeDtypeStruct((CH, TOK, D), bf16),
            jax.ShapeDtypeStruct((2 * NY, CH, 8, D), bf16),
            jax.ShapeDtypeStruct((CH, 16, 128), bf16),
        ),
        in_specs=[vmem, vmem, vmem],
        out_specs=(any_, any_, any_),
        scratch_shapes=[
            dma((3,)),
            dma((2, PARTS)),
            dma((2, PARTS)),
            dma((4, 3, PARTS)),
            dma((4, 3, PARTS)),
            dma((2, 11)),
            dma((2, 11)),
            dma((2, 4, 2)),
            dma((2, 4, 2)),
            dma((3, 4, 2)),
            dma((3, 4, 2)),
        ],
        compiler_params=pltpu.CompilerParams(collective_id=0, has_side_effects=True),
        name="gather_all",
    )(tok, wp, kt)


OWN = NY * NL


def sum_kernel(g, out, half_in, held, mine, acc, s0, r0, s1, r1, s2, r2, s3, r3):
    dp, ch = coords()
    core, own = dp % 2, dp // 2
    sib = (own * 2 + 1 - core, ch)

    barrier = pltpu.get_barrier_semaphore()

    @pl.loop(1, OWN)
    def _(j):
        pl.semaphore_signal(
            barrier, inc=1, device_id=(((own + j) % OWN) * 2 + core, ch), device_id_type=MESH
        )

    pl.semaphore_signal(barrier, inc=1, device_id=sib, device_id_type=MESH)
    pl.semaphore_wait(barrier, OWN)

    def remote(src, dst, ss, rs, dev):
        return pltpu.make_async_remote_copy(
            src_ref=src, dst_ref=dst, send_sem=ss, recv_sem=rs, device_id=dev, device_id_type=MESH
        )

    pair = remote(g.at[1 - core], half_in, s0, r0, sib)
    pair.start()
    pair.wait_recv()
    acc[...] = (g[core].astype(f32) + half_in[...].astype(f32)).astype(bf16)

    @pl.loop(1, OWN)
    def _(j):
        to = (own + j) % OWN
        remote(acc.at[to], held.at[own], s1.at[to], r1.at[own], (to * 2 + core, ch)).start()

    total = acc[own].astype(f32)

    def add(j, total):
        at = (own + OWN - j) % OWN
        remote(acc.at[at], held.at[at], s1.at[at], r1.at[at], sib).wait_recv()
        return total + held[at].astype(f32)

    total = lax.fori_loop(1, OWN, add, total)
    mine[...] = total.astype(bf16)

    @pl.loop(1, OWN)
    def _(j):
        to = (own + j) % OWN
        remote(mine, out.at[core, own], s2.at[to], r2.at[own], (to * 2 + core, ch)).start()

    put = pltpu.make_async_copy(mine, out.at[core, own], s3.at[1])
    put.start()

    @pl.loop(1, OWN)
    def _(j):
        at = (own + OWN - j) % OWN
        remote(mine, out.at[core, at], s2.at[at], r2.at[at], sib).wait_recv()

    put.wait()
    back = remote(out.at[core], out.at[core], s3.at[0], r3, sib)
    back.start()
    remote(out.at[1 - core], out.at[1 - core], s3.at[0], r3, sib).wait_recv()
    back.wait_send()
    pair.wait_send()

    @pl.loop(1, OWN)
    def _(j):
        to = (own + j) % OWN
        remote(acc.at[to], held.at[own], s1.at[to], r1.at[own], sib).wait_send()
        remote(mine, out.at[core, own], s2.at[to], r2.at[own], sib).wait_send()


def sum_over_dp(g):
    vmem = pl.BlockSpec(memory_space=pltpu.VMEM)
    dma = pltpu.SemaphoreType.DMA
    shape = (OWN, 8, LANES)
    return pl.pallas_call(
        sum_kernel,
        out_shape=jax.ShapeDtypeStruct((2, *shape), bf16),
        in_specs=[vmem],
        out_specs=vmem,
        scratch_shapes=[
            pltpu.VMEM(shape, bf16),
            pltpu.VMEM(shape, bf16),
            pltpu.VMEM(shape[1:], bf16),
            pltpu.VMEM(shape, bf16),
            dma,
            dma,
            dma((OWN,)),
            dma((OWN,)),
            dma((OWN,)),
            dma((OWN,)),
            dma((2,)),
            dma,
        ],
        compiler_params=pltpu.CompilerParams(collective_id=1, has_side_effects=True),
        name="sum_over_dp",
    )(g)


def split(value):
    high = lax.reduce_precision(value, 8, 7)
    return high.astype(bf16), (value - high).astype(bf16)


def dot(a, b, ca, cb):
    return lax.dot_general(a, b, (((ca,), (cb,)), ((), ())), preferred_element_type=f32)


def per_device(
    pixels,
    embed_weight,
    channel_bias,
    agg_query,
    key_weight,
    value_weight,
    final_query,
    out_weight,
    group_counts,
    grad_output,
):
    dp, ch = coords()
    channels, pixel_count = embed_weight.shape[:2]
    query_row = agg_query[0]
    query_head = final_query[0].astype(f32)

    patches = pixels.reshape(TOK, channels, pixel_count)
    embedded = (
        jnp.einsum("tcp,cpd->tcd", patches, embed_weight, preferred_element_type=f32)
        + channel_bias.astype(f32)[None]
    ).astype(bf16)
    live_mask = (jnp.arange(channels, dtype=jnp.int32) < group_counts[0]).astype(f32)
    agg_capped = CAP * jnp.tanh(
        jnp.einsum("tcd,d->tc", embedded, query_row, preferred_element_type=f32) / CAP
    )
    agg_exp = jnp.exp(agg_capped) * live_mask[None]
    agg_weight = agg_exp / jnp.sum(agg_exp, -1, keepdims=True)
    agg_round = agg_weight.astype(bf16)
    group_token = jnp.einsum(
        "tc,tcd->td", agg_round, embedded, preferred_element_type=f32
    ).astype(bf16)

    key_query = jnp.sum(key_weight.astype(f32) * query_head[None], 1)
    kq_high, kq_low = split(key_query)
    kt = jnp.concatenate([kq_high.reshape(8, 128), kq_low.reshape(8, 128)], 0)
    shard = jnp.concatenate([value_weight.T, out_weight], 0)
    piece = lax.dynamic_slice_in_dim(shard, (dp % 16) * 8, 8, 0)
    tokens, weights, kts = gather_all(group_token, piece, kt)
    flat = tokens.reshape(CH * TOK, D)
    all_value = weights[:NY].reshape(HEADS * HD, D)
    all_out = weights[NY:].reshape(HEADS * HD, D)
    kts = kts.reshape(HEADS, 2, D)
    kt_high, kt_low = kts[:, 0], kts[:, 1]

    column_head = (jnp.arange(HEADS * HD) // 8) % HEADS
    expand = (column_head[None] == jnp.arange(HEADS)[:, None]).astype(bf16)
    scores = dot(flat, jnp.concatenate([kt_high, kt_low], 0), 1, 1)
    scores = (scores[:, :HEADS] + scores[:, HEADS:]).reshape(CH, TOK, HEADS)
    tanh = jnp.tanh(scores / 8.0 / CAP)
    head_exp = jnp.exp(CAP * tanh)
    head_prob = head_exp / jnp.sum(head_exp, 0, keepdims=True)
    head_round = head_prob.astype(bf16)
    values = dot(flat, all_value, 1, 1).astype(bf16)
    spread = dot(head_round.reshape(CH * TOK, HEADS), expand, 1, 0)
    attended = jnp.sum((spread * values.astype(f32)).reshape(CH, TOK, HEADS * HD), 0).astype(bf16)
    layer_out = dot(attended, all_out, 1, 0).astype(bf16)
    attended_grad = dot(grad_output, all_out, 1, 1).astype(bf16)
    product = values.reshape(CH, TOK, HEADS * HD).astype(f32) * attended_grad.astype(f32)[None]
    high, low = split(product.reshape(CH * TOK, HEADS * HD))
    prob_grad = (dot(high, expand, 1, 1) + dot(low, expand, 1, 1)).reshape(CH, TOK, HEADS)
    score_grad = head_prob * (prob_grad - jnp.sum(head_prob * prob_grad, 0, keepdims=True))
    raw_grad = score_grad * (1.0 - tanh**2) / 8.0

    my_round = lax.dynamic_index_in_dim(head_round, ch, 2, False)
    my_raw = lax.dynamic_index_in_dim(raw_grad, ch, 2, False)
    my_values = dot(flat, value_weight, 1, 0).astype(bf16).reshape(CH, TOK, HD)
    my_attended = jnp.sum(my_round.astype(f32)[..., None] * my_values.astype(f32), 0).astype(bf16)
    my_grad = dot(grad_output, out_weight, 1, 1).astype(bf16)
    grad_out = dot(my_attended, grad_output, 0, 0)
    value_grad = (my_round.astype(f32)[..., None] * my_grad.astype(f32)[None]).astype(bf16)
    raw_high, raw_low = split(my_raw.reshape(CH * TOK, 1))
    left = jnp.concatenate([value_grad.reshape(CH * TOK, HD), raw_high, raw_low], 1)
    of_tokens = dot(left, flat, 0, 0)

    group_raw = lax.dynamic_index_in_dim(raw_grad, ch, 0, False)
    group_spread = lax.dynamic_slice_in_dim(spread, ch * TOK, TOK, 0)
    group_high, group_low = split(group_raw)
    group_value = (group_spread * attended_grad.astype(f32)).astype(bf16)
    token_grad = dot(group_value, all_value, 1, 0) + dot(
        jnp.concatenate([group_high, group_low, group_high], 1),
        jnp.concatenate([kt_high, kt_high, kt_low], 0),
        1,
        0,
    )
    mix_grad = jnp.einsum("td,tcd->tc", token_grad, embedded.astype(f32))
    mix_weighted = jnp.sum(agg_weight * mix_grad, -1, keepdims=True)
    agg_raw_grad = agg_weight * (mix_grad - mix_weighted) * (1.0 - (agg_capped / CAP) ** 2)
    embed_grad = (
        agg_round.astype(f32)[:, :, None] * token_grad[:, None, :]
        + agg_raw_grad[:, :, None] * query_row.astype(f32)[None, None, :]
    ).astype(bf16)
    grad_agg = jnp.einsum("tc,tcd->d", agg_raw_grad, embedded.astype(f32))[None]
    grad_embed = jnp.einsum("tcp,tcd->cpd", patches, embed_grad, preferred_element_type=f32)
    grad_bias = jnp.sum(embed_grad.astype(f32), 0)

    large = jnp.concatenate(
        [grad_embed.reshape(channels * pixel_count, D), of_tokens[:HD], grad_out], 0
    ).reshape(OWN, 8, D)
    u_row = (of_tokens[HD] + of_tokens[HD + 1])[None]
    few = jnp.concatenate([grad_bias, grad_agg, u_row], 0).reshape(80, 128)
    few = jnp.pad(few, ((0, OWN * 8 - 80), (0, 0))).reshape(OWN, 8, 128)
    packed = jnp.stack(
        [
            jnp.concatenate([large[:, :, :512], few], 2),
            jnp.concatenate([large[:, :, 512:], jnp.zeros_like(few)], 2),
        ]
    ).astype(bf16)
    summed = sum_over_dp(packed).astype(f32)
    large = jnp.concatenate([summed[0, :, :, :512], summed[1, :, :, :512]], 2).reshape(OWN * 8, D)
    few = summed[0, :, :, 512:].reshape(OWN * 8, 128)[:80].reshape(10, D)
    u_row = few[9]
    grad_key = u_row[:, None] * query_head[None]
    grad_query = jnp.sum(u_row[:, None] * key_weight.astype(f32), 0)[None]
    return (
        layer_out,
        large[:128].reshape(channels, pixel_count, D),
        few[:8],
        few[8:9],
        grad_key,
        large[128:192].T,
        grad_query,
        large[192:],
    )


def solution(mesh):
    in_specs = (
        P("dp", "chan"),
        P("chan", None, None),
        P("chan", None),
        P("chan", None),
        P(None, "chan"),
        P(None, "chan"),
        P("chan", None),
        P("chan", None),
        P("chan"),
        P("dp", None),
    )
    out_specs = (
        P("dp", None),
        P("chan", None, None),
        P("chan", None),
        P("chan", None),
        P(None, "chan"),
        P(None, "chan"),
        P("chan", None),
        P("chan", None),
    )
    return jax.shard_map(
        per_device, mesh=mesh, in_specs=in_specs, out_specs=out_specs, check_vma=False
    )
```

time: 761 us -> 166 us (0.22)
  waiting for transfers between devices: 434 us -> 0 us
  blocking collectives: 265 us -> 0 us
  Pallas kernels: 0 us -> 101 us
  starting transfers between devices: 14.3 us -> 0 us
  between operations: 14.7 us -> 1.86 us
  other arithmetic: 3.8 us -> 15.9 us
  matrix products: 16.7 us -> 25.8 us
  local copies, waits for them, and re-layouts: 11.4 us -> 20.2 us
    psum x1 -> x0, blocking collectives: 265 us -> none  [per_device(): lax.psum((grad_embed, grad_bias, grad_agg, grad_key, grad_value, grad_que...]
    psum x1 -> x0, waiting for transfers between devices: 249 us -> none  [per_device(): lax.psum((grad_embed, grad_bias, grad_agg, grad_key, grad_value, grad_que...]
    pallas_call x0 -> x2, Pallas kernels: none -> 101 us  [the longest x1 54.7 us: gather_all(): pl.pallas_call(gather_kernel, out_shape=(jax.ShapeDtypeStruct((CH, TOK, D...]
    all_gather x1 -> x0, waiting for transfers between devices: 97.1 us -> none  [per_device(): gathered = lax.all_gather(group_token[:, None, :], CHAN, axis=1, tiled=True)]
    reduce_scatter x2 -> x0, waiting for transfers between devices: 76 us -> none  [sum_by_axis(): shard = lax.psum_scatter(shard, axis, scatter_dimension=dim, tiled=True)]
    all_to_all x2 -> x0, starting transfers between devices: 14.1 us -> none  [the longest x1 8.76 us: summed_on_arrival(): lax.all_to_all(in_blocks(shard, dim, devices), axis, 0, 0, tiled=True)]
    all_to_all x2 -> x0, waiting for transfers between devices: 11.5 us -> none  [the longest x1 11.5 us: from_everyone(): lax.all_to_all(jnp.broadcast_to(shard[None], (devices, *shard.shape)), ax...]
    dot_general x14 -> x18, matrix products: 16.1 us -> 25.2 us  [the longest x13 19.1 us: dot(): lax.dot_general(a, b, (((ca,), (cb,)), ((), ())), preferred_element_type=...]
  transfers between devices with their start and end apart: 6 -> 0, of which waited for: 5 -> 0; matrix products, arithmetic and copies ran while one was open for 2% -> 0% of each run, Pallas kernels for 0% -> 0%
where the time goes in v1:
time: 166 us; the launch traced here: 164 us
  Pallas kernels  101 us (61%)
  matrix products  25.8 us (16%)
  local copies, waits for them, and re-layouts  20.2 us (12%)
  other arithmetic  15.9 us (10%)
  between operations  1.86 us (1%)
    pallas_call x1, Pallas kernels, gather_all(): pl.pallas_call(gather_kernel, out_shape=(jax.ShapeDtypeStruct((CH, TOK, D...  54.7 us
    pallas_call x1, Pallas kernels, sum_over_dp(): pl.pallas_call(sum_kernel, out_shape=jax.ShapeDtypeStruct((2, *shape), bf...  46 us
    dot_general x13, matrix products, dot(): lax.dot_general(a, b, (((ca,), (cb,)), ((), ())), preferred_element_type=...  19.1 us
    unnamed x73, local copies, waits for them, and re-layouts  8.4 us

profile of v1, /device:TPU:1, one launch (start us, length us, event | category | flops | bytes accessed | tf_op | source)
XLA Modules:
  0.0 164.4 jit_solution(5529100334848149629)
XLA Ops:
  0.7 1.4 fusion.55.wp
  6.8 1.1 fusion.12
  9.9 54.7 %gather_all.1 = (bf16[12,96,1024]{2,1,0:T(8,128)(2,1)}, bf16[16,12,8,1024]{3,2,1,0:T(8,128)(2,1)}, bf16[12,16,128]{2,1,0:T(8,128)(2,1)}) custom-call(bf16[96,1024]{1,0:T(8,128)(2,1)} %bitcast.142, bf16[8,1024]{1,0:T(8,128)(2,1)} %fusion.55.wp, bf16[16,128]{1,0:T(8,128)(2,1)} %pad_maximum_fusion.3.kt), custom_call_target="tpu_custom_call" | custom-call | tf_op jit(solution)/shard_map/gather_all/pallas_call | solution.py:186
  65.6 2.4 %fusion.46 = f32[1152,24]{0,1:T(8,128)S(1)} fusion(bf16[1152,1024]{1,0:T(8,128)(2,1)} %bitcast.132, bf16[12,1024]{1,0:T(8,128)(2,1)S(1)} %get-tuple-element.39, bf16[12,1024]{1,0:T(8,128)(2,1)S(1)} %get-tuple-element.40), kind=kOutput, calls=%fused_computation.85 | convolution fusion | flops 56721408 | bytes 2519040 | tf_op jit(solution)/shard_map/dot_general | solution.py:318
  69.6 1.8 %copy-done.8 = bf16[16,12,8,1024]{3,2,1,0:T(8,128)(2,1)S(1)} copy-done((bf16[16,12,8,1024]{3,2,1,0:T(8,128)(2,1)S(1)}, bf16[16,12,8,1024]{3,2,1,0:T(8,128)(2,1)}, u32[]{:S(2)}) %copy-start.8) | copy-done | bytes 3145752
  71.8 1.2 copy-done.6
  74.3 4.1 %fusion.1 = (bf16[1152,768]{1,0:T(8,128)(2,1)S(1)}, bf16[1152,768]{1,0:T(8,128)(2,1)S(1)}, f32[1152,768]{1,0:T(8,128)}) fusion(f32[96,768]{1,0:T(8,128)S(1)} %fusion.15, f32[1152,768]{1,0:T(8,128)S(1)} %fusion.51, bf16[1152,1024]{1,0:T(8,128)(2,1)S(1)} %bitcast.133, bf16[768,1024]{1,0:T(8,128)(2,1)S(1)} %bitcast.137), kind=kOutput, calls=%fused_computation.5 | convolution fusion | flops 1819017216 | bytes 14843904 | tf_op jit(solution)/shard_map/dot_general | solution.py:318
  78.9 1.2 convolution_add_fusion
  80.2 1.0 reshape.178
  83.5 1.0 fusion.38
  84.5 2.1 %convolution_add_fusion.1 = f32[96,1024]{1,0:T(8,128)S(1)} fusion(f32[96,1024]{1,0:T(8,128)} %fusion.38, bf16[768,1024]{1,0:T(8,128)(2,1)} %bitcast.138, f32[96,768]{1,0:T(8,128)S(1)} %fusion.15, f32[1152,768]{1,0:T(8,128)} %copy-done.2, s32[]{:T(128)S(6)} %select_n.52), kind=kOutput, calls=%fused_computation.27 | convolution fusion | flops 151240704 | bytes 2949124 | tf_op jit(solution)/shard_map/dot_general | solution.py:318
  86.6 1.4 fusion.10
  88.2 1.2 fusion.3
  89.4 1.8 %fusion.89 = f32[1,1024,1]{1,0,2:T(1,128)S(1)} fusion(f32[96,8,1]{0,2,1:T(1,128)S(1)} %bitcast.152, bf16[96,8,1024]{2,0,1:T(8,128)(2,1)} %copy-done.3), kind=kOutput, calls=%fused_computation.160 | convolution fusion | flops 1572864 | bytes 1580032 | tf_op jit(solution)/shard_map/tc,tcd->d/dot_general | solution.py:413
  95.1 1.7 %fusion.20 = f32[96,64]{0,1:T(8,128)} fusion(bf16[96,1024]{1,0:T(8,128)(2,1)S(1)} %copy-done.9, bf16[64,1024]{1,0:T(8,128)(2,1)} %param.17), kind=kOutput, calls=%fused_computation.37 | convolution fusion | flops 12595200 | bytes 352256 | tf_op jit(solution)/shard_map/dot_general | solution.py:318
  98.7 1.7 %fusion.25 = f32[66,1024]{1,0:T(8,128)S(1)} fusion(bf16[1152,1024]{1,0:T(8,128)(2,1)S(1)} %bitcast.134, bf16[1152,1]{1,0:T(8,128)(2,1)} %copy.33, bf16[1152,1]{1,0:T(8,128)(2,1)S(1)} %copy.32, bf16[1152,64]{1,0:T(8,128)(2,1)S(1)} %fusion.21), kind=kOutput, calls=%fused_computation.53 | convolution fusion | flops 156169728 | bytes 2781696 | tf_op jit(solution)/shard_map/dot_general | solution.py:318
  102.1 1.3 fusion.4
  105.0 1.8 %fusion.2 = f32[1152,64]{0,1:T(8,128)S(1)} fusion(bf16[1152,1024]{1,0:T(8,128)(2,1)S(1)} %bitcast.135, bf16[1024,64]{0,1:T(8,128)(2,1)} %param.15), kind=kOutput, calls=%fused_computation.10 | convolution fusion | flops 151142400 | bytes 2785280 | tf_op jit(solution)/shard_map/dot_general | solution.py:318
  108.6 46.0 %sum_over_dp.1 = bf16[2,32,8,640]{3,2,1,0:T(8,128)(2,1)} custom-call(bf16[2,32,8,640]{3,2,1,0:T(8,128)(2,1)} %pad_maximum_fusion.g), custom_call_target="tpu_custom_call" | custom-call | tf_op jit(solution)/shard_map/sum_over_dp/pallas_call | solution.py:288
  154.6 1.2 convert_element_type.193
  157.6 1.4 fusion.32
  159.6 1.3 slice.117
  160.9 2.3 %reduce_sum.87 = bf16[96,768]{1,0:T(8,128)(2,1)S(1)} reduce(f32[12,96,768]{2,1,0:T(8,128)} %bitcast.136, f32[]{:T(128)} %constant.72.clone.1), dimensions={0}, to_apply=%region_3.4 | reduce | flops 811008 | bytes 3686404 | tf_op jit(solution)/shard_map/reduce_sum | solution.py:376
  163.4 1.1 convolution_convert_fusion.2
  (135 shorter events, 26.6 us)
Async XLA Ops:
  0.6 3.0 %copy-start = (bf16[8,16,1024]{2,1,0:T(8,128)(2,1)S(1)}, bf16[8,16,1024]{2,1,0:T(8,128)(2,1)}, u32[]{:S(2)}) copy-start(bf16[8,16,1024]{2,1,0:T(8,128)(2,1)} %param.11) | copy-start | bytes 786436
  0.6 3.6 %copy-start.26 = (bf16[1,1024]{1,0:T(2,128)(2,1)S(1)}, bf16[1,1024]{1,0:T(2,128)(2,1)}, u32[]{:S(2)}) copy-start(bf16[1,1024]{1,0:T(2,128)(2,1)} %param.13) | copy-start | bytes 6148
  4.3 3.6 %copy-start.3 = (bf16[96,8,1024]{2,0,1:T(8,128)(2,1)}, bf16[96,8,1024]{2,0,1:T(8,128)(2,1)S(1)}, u32[]{:S(2)}) copy-start(bf16[96,8,1024]{2,0,1:T(8,128)(2,1)S(1)} %fusion.9) | copy-start | bytes 4718596
  4.3 4.4 %copy-start.34 = (bf16[1,64]{1,0:T(2,128)(2,1)S(1)}, bf16[1,64]{1,0:T(2,128)(2,1)}, u32[]{:S(2)}) copy-start(bf16[1,64]{1,0:T(2,128)(2,1)} %param.16) | copy-start | bytes 388
  4.3 4.9 %copy-start.11 = (bf16[1024,64]{0,1:T(8,128)(2,1)S(1)}, bf16[1024,64]{0,1:T(8,128)(2,1)}, u32[]{:S(2)}) copy-start(bf16[1024,64]{0,1:T(8,128)(2,1)} %param.14) | copy-start | bytes 393220
  68.9 2.5 %copy-start.8 = (bf16[16,12,8,1024]{3,2,1,0:T(8,128)(2,1)S(1)}, bf16[16,12,8,1024]{3,2,1,0:T(8,128)(2,1)}, u32[]{:S(2)}) copy-start(bf16[16,12,8,1024]{3,2,1,0:T(8,128)(2,1)} %get-tuple-element.13) | copy-start | bytes 9437188
  69.6 3.9 %copy-start.2 = (f32[1152,768]{1,0:T(8,128)}, f32[1152,768]{1,0:T(8,128)S(1)}, u32[]{:S(2)}) copy-start(f32[1152,768]{1,0:T(8,128)S(1)} %fusion.51) | copy-start | bytes 10616836
  71.4 2.9 %copy-start.1 = (bf16[12,96,1024]{2,1,0:T(8,128)(2,1)S(1)}, bf16[12,96,1024]{2,1,0:T(8,128)(2,1)}, u32[]{:S(2)}) copy-start(bf16[12,96,1024]{2,1,0:T(8,128)(2,1)} %get-tuple-element.11) | copy-start | bytes 7077892
  71.7 6.6 %copy-start.5 = (bf16[8,12,8,1024]{3,2,1,0:T(8,128)(2,1)}, bf16[8,12,8,1024]{3,2,1,0:T(8,128)(2,1)S(1)}, u32[]{:S(2)}) copy-start(bf16[8,12,8,1024]{3,2,1,0:T(8,128)(2,1)S(1)} %get-tuple-element.14) | copy-start | bytes 4718596
  81.9 2.6 %copy-start.13 = (f32[12,96,12]{1,0,2:T(8,128)}, f32[12,96,12]{1,0,2:T(8,128)S(1)}, u32[]{:S(2)}) copy-start(f32[12,96,12]{1,0,2:T(8,128)S(1)} %broadcast_divide_fusion) | copy-start | bytes 165892
  84.5 2.1 %copy-start.4 = (bf16[96,8,1024]{2,0,1:T(8,128)(2,1)S(1)}, bf16[96,8,1024]{2,0,1:T(8,128)(2,1)}, u32[]{:S(2)}) copy-start(bf16[96,8,1024]{2,0,1:T(8,128)(2,1)} %copy-done.3) | copy-start | bytes 4718596
  88.1 4.4 %copy-start.22 = (f32[96,8]{0,1:T(8,128)}, f32[96,8]{0,1:T(8,128)S(1)}, u32[]{:S(2)}) copy-start(f32[96,8]{0,1:T(8,128)S(1)} %get-tuple-element.31) | copy-start | bytes 9220
  88.2 7.0 %copy-start.20 = (f32[96,8]{0,1:T(8,128)}, f32[96,8]{0,1:T(8,128)S(1)}, u32[]{:S(2)}) copy-start(f32[96,8]{0,1:T(8,128)S(1)} %fusion.77) | copy-start | bytes 9220
  88.2 4.3 %copy-start.24 = (f32[1024]{0:T(1024)}, f32[1024]{0:T(1024)S(1)}, u32[]{:S(2)}) copy-start(f32[1024]{0:T(1024)S(1)} %convert_element_type.179) | copy-start | bytes 12292
  98.6 2.5 %copy-start.19 = (bf16[8,1024]{1,0:T(8,128)(2,1)S(1)}, bf16[8,1024]{1,0:T(8,128)(2,1)}, u32[]{:S(2)}) copy-start(bf16[8,1024]{1,0:T(8,128)(2,1)} %fusion.3) | copy-start | bytes 49156
  98.6 2.5 %copy-start.27 = (bf16[1,1024]{1,0:T(2,128)(2,1)S(1)}, bf16[1,1024]{1,0:T(2,128)(2,1)}, u32[]{:S(2)}) copy-start(bf16[1,1024]{1,0:T(2,128)(2,1)} %broadcast_in_dim.5) | copy-start | bytes 6148
  98.6 3.4 %copy-start.17 = (bf16[96,128]{0,1:T(8,128)(2,1)S(1)}, bf16[96,128]{0,1:T(8,128)(2,1)}, u32[]{:S(2)}) copy-start(bf16[96,128]{0,1:T(8,128)(2,1)} %copy-done.16) | copy-start | bytes 73732
  98.6 3.4 %copy-start.21 = (f32[96,8]{0,1:T(8,128)S(1)}, f32[96,8]{0,1:T(8,128)}, u32[]{:S(2)}) copy-start(f32[96,8]{0,1:T(8,128)} %copy-done.20) | copy-start | bytes 9220
  98.7 3.4 %copy-start.23 = (f32[96,8]{0,1:T(8,128)S(1)}, f32[96,8]{0,1:T(8,128)}, u32[]{:S(2)}) copy-start(f32[96,8]{0,1:T(8,128)} %copy-done.22) | copy-start | bytes 9220
  98.7 3.4 %copy-start.25 = (f32[1024]{0:T(1024)S(1)}, f32[1024]{0:T(1024)}, u32[]{:S(2)}) copy-start(f32[1024]{0:T(1024)} %copy-done.24) | copy-start | bytes 12292
  105.0 2.4 %copy-start.15 = (bf16[8,1024,16]{1,2,0:T(8,128)(2,1)S(1)}, bf16[8,1024,16]{1,2,0:T(8,128)(2,1)}, u32[]{:S(2)}) copy-start(bf16[8,1024,16]{1,2,0:T(8,128)(2,1)} %fusion.4) | copy-start | bytes 786436
  155.9 1.7 %copy-start.12 = (bf16[1024,64]{0,1:T(8,128)(2,1)S(1)}, bf16[1024,64]{0,1:T(8,128)(2,1)}, u32[]{:S(2)}) copy-start(bf16[1024,64]{0,1:T(8,128)(2,1)} %param.14) | copy-start | bytes 393220
  155.9 1.7 %copy-start.33 = (f32[64]{0:T(128)S(1)}, f32[64]{0:T(128)}, u32[]{:S(2)}) copy-start(f32[64]{0:T(128)} %copy-done.32) | copy-start | bytes 772
  160.9 2.5 %copy-start.7 = (bf16[8,12,8,1024]{3,2,1,0:T(8,128)(2,1)S(1)}, bf16[8,12,8,1024]{3,2,1,0:T(8,128)(2,1)}, u32[]{:S(2)}) copy-start(bf16[8,12,8,1024]{3,2,1,0:T(8,128)(2,1)} %copy-done.6) | copy-start | bytes 4718596
  (11 other events, 10.1 us)

commit v2 on v1

v2 whole, which is shorter than its diff:
```python
import jax
import jax.numpy as jnp
from jax import lax
from jax.experimental import pallas as pl
from jax.experimental.pallas import tpu as pltpu
from jax.sharding import PartitionSpec as P

MESH = pl.DeviceIdType.MESH
NX, NH, NY, NL = 4, 3, 8, 4
CH = NX * NH
TOK, D = 96, 1024
HEADS, HD = 12, 64
WIDE = HEADS * HD
CHANNELS, PP = 8, 16
PARTS = 3
PR = TOK // PARTS
PH = PR // 2
CAP = 15.0
LANES = 640
OWN = NY * NL

f32, bf16 = jnp.float32, jnp.bfloat16


def dot(a, b, ca, cb):
    return lax.dot_general(a, b, (((ca,), (cb,)), ((), ())), preferred_element_type=f32)


def iota(shape, dim):
    return lax.broadcasted_iota(jnp.int32, shape, dim)


def split(value):
    high = value.astype(bf16)
    return high, (value - high.astype(f32)).astype(bf16)


def stacked(row):
    at = iota((8, 128), 0)
    out = jnp.zeros((8, 128), f32)
    for j in range(8):
        out = jnp.where(at == j, row[:, 128 * j : 128 * j + 128], out)
    return out


def step_kernel(
    pix,
    wemb,
    bias,
    aggq,
    kw,
    vw,
    fq,
    outw,
    counts,
    go,
    layer,
    out,
    emb,
    tok_all,
    w_all,
    kt_all,
    tok,
    wp,
    kt,
    head_v,
    head_o,
    kq,
    val,
    left,
    th_s,
    hp_s,
    pg_s,
    g,
    half_in,
    held,
    mine,
    acc,
    sz,
    rz,
    sx,
    rx,
    sw,
    rw,
    sy,
    ry,
    sb,
    rb,
    s0,
    r0,
    s1,
    r1,
    s2,
    r2,
    s3,
    r3,
    s4,
):
    dp, ch = lax.axis_index("dp"), lax.axis_index("chan")
    x, zh = ch // NH, ch % NH
    core, own = dp % 2, dp // 2
    y, zl = own % NY, own // NY
    xn, xp = (x + 1) % NX, (x + NX - 1) % NX
    yn, yp = (y + 1) % NY, (y + NY - 1) % NY

    def at_chan(x_, z_):
        return (dp, x_ * NH + z_)

    def at_dp(y_, c_):
        return (zl * (2 * NY) + y_ * 2 + c_, ch)

    zdev = [at_chan(x, (zh + k + 1) % NH) for k in range(2)]
    xdev = [at_chan(xn, zh), at_chan(xp, zh)]
    ydev = [at_dp(yn, core), at_dp(yp, core)]
    sib = at_dp(y, 1 - core)

    barrier = pltpu.get_barrier_semaphore()
    for dev in zdev + xdev + [sib]:
        pl.semaphore_signal(barrier, inc=1, device_id=dev, device_id_type=MESH)

    @pl.loop(1, OWN)
    def _(j):
        pl.semaphore_signal(
            barrier, inc=1, device_id=(((own + j) % OWN) * 2 + core, ch), device_id_type=MESH
        )

    lane = iota((TOK, 128), 1)
    pixels = pix[...]
    query = aggq[...].astype(f32)
    score = jnp.zeros((TOK, 128), f32)
    for c in range(CHANNELS):
        masked = jnp.where((lane >= PP * c) & (lane < PP * (c + 1)), pixels, jnp.zeros_like(pixels))
        e = (dot(masked, wemb[...], 1, 0) + bias[c : c + 1, :].astype(f32)).astype(bf16)
        emb[c] = e
        s = jnp.sum(e.astype(f32) * query, 1, keepdims=True)
        score = jnp.where(lane == c, s, score)
    capped = CAP * jnp.tanh(score / CAP)
    agg_exp = jnp.exp(capped) * jnp.where(lane < counts[...], 1.0, 0.0)
    agg_weight = agg_exp / jnp.sum(agg_exp, 1, keepdims=True)
    agg_round = agg_weight.astype(bf16).astype(f32)
    token = jnp.zeros((TOK, D), f32)
    for c in range(CHANNELS):
        token += agg_round[:, c : c + 1] * emb[c].astype(f32)
    tok[...] = token.astype(bf16)
    tok_all[pl.ds(pl.multiple_of(ch * TOK, 32), TOK), :] = tok[...]

    eye = (iota((128, 128), 0) == iota((128, 128), 1)).astype(f32).astype(bf16)
    flipped = dot(eye[:HD, :HD], vw[...], 1, 1)
    head_v[:HD] = flipped.astype(bf16)
    head_v[HD:] = jnp.zeros((HD, D), bf16)
    head_o[:HD] = outw[...]
    head_o[HD:] = jnp.zeros((HD, D), bf16)
    for q in range(4):
        wp[q] = head_v[16 * q : 16 * q + 16, :]
        wp[4 + q] = outw[16 * q : 16 * q + 16, :]
    fq8 = jnp.broadcast_to(fq[...].astype(f32), (16, HD)).astype(bf16)
    kt[...] = stacked(dot(fq8, kw[...], 1, 1)[:1])
    kt_all[ch] = kt[...]

    started = []

    def remote(src, dst, ss, rs, dev):
        return pltpu.make_async_remote_copy(
            src_ref=src, dst_ref=dst, send_sem=ss, recv_sem=rs, device_id=dev, device_id_type=MESH
        )

    def send(src, dst, ss, rs, dev):
        copy = remote(src, dst, ss, rs, dev)
        copy.start()
        started.append(copy)

    def arrive(dst, ss, rs):
        remote(dst, dst, ss, rs, sib).wait_recv()

    def owner(dx, k):
        return ((x + NX - dx) % NX) * NH + (zh + NH - k) % NH

    def at_rows(c, start, rows):
        return tok_all.at[pl.ds(pl.multiple_of(c * TOK + start, 16), rows)]

    lanes = pl.multiple_of(core * 512, 512)
    wmine = wp.at[y, :, pl.ds(lanes, 512)]

    def piece(c):
        return w_all.at[pl.ds(pl.multiple_of((y * CH + c) * 16, 16), 16), pl.ds(lanes, 512)]

    small = [(wmine, piece), (kt, lambda c: kt_all.at[c])]

    def part(c, p):
        return at_rows(c, p * PR, PR)

    def half(c, p, h):
        return at_rows(c, p * PR + h * PH, PH)

    place = pltpu.make_async_copy(wmine, piece(ch), s4)
    place.start()
    pl.semaphore_wait(barrier, OWN + 4)

    for i, (src, dst) in enumerate(small):
        for k in range(2):
            send(src, dst(ch), sw.at[i, k], rw.at[i, k], zdev[k])
        for d in range(2):
            send(src, dst(ch), sw.at[i, 2 + 3 * d], rw.at[i, 2 + 3 * d], xdev[d])
    for p in range(PARTS):
        own_part = tok.at[pl.ds(p * PR, PR)]
        for k in range(2):
            send(own_part, part(ch, p), sz.at[k, p], rz.at[k, p], zdev[k])
        for d in range(2):
            send(own_part, part(ch, p), sx.at[d, 0, p], rx.at[d, 0, p], xdev[d])

    place.wait()

    for k in (1, 2):
        for i, (_, dst) in enumerate(small):
            c = owner(0, k)
            arrive(dst(c), sw.at[i, k - 1], rw.at[i, k - 1])
            for d in range(2):
                send(dst(c), dst(c), sw.at[i, 2 + 3 * d + k], rw.at[i, 2 + 3 * d + k], xdev[d])
    for k in range(3):
        for i, (_, dst) in enumerate(small):
            c = owner(1, k)
            arrive(dst(c), sw.at[i, 2 + k], rw.at[i, 2 + k])
            send(dst(c), dst(c), sw.at[i, 8 + k], rw.at[i, 8 + k], xdev[0])

    def relay(k, p):
        c = owner(1, k)
        arrive(part(c, p), sx.at[0, k, p], rx.at[0, k, p])
        send(half(c, p, 0), half(c, p, 0), sx.at[2, k, p], rx.at[2, k, p], xdev[0])
        c = owner(NX - 1, k)
        arrive(part(c, p), sx.at[1, k, p], rx.at[1, k, p])
        send(half(c, p, 1), half(c, p, 1), sx.at[3, k, p], rx.at[3, k, p], xdev[1])

    for p in range(PARTS):
        relay(0, p)
    for k in range(3):
        for i, (_, dst) in enumerate(small):
            c = owner(NX - 1, k)
            arrive(dst(c), sw.at[i, 5 + k], rw.at[i, 5 + k])
            c = owner(2, k)
            arrive(dst(c), sw.at[i, 8 + k], rw.at[i, 8 + k])

    def rows_of(y_, h, core_):
        at = ((y_ + 2 * NY) % NY) * (CH * 16) + h * 96
        return w_all.at[
            pl.ds(pl.multiple_of(at, 32), 96), pl.ds(pl.multiple_of(core_ * 512, 512), 512)
        ]

    def sub(y_, h):
        return rows_of(y_, h, core)

    def ysend(s, h, d):
        block = sub(y - s, h) if d == 0 else sub(y + s, h)
        send(block, block, sy.at[d, s, h], ry.at[d, s, h], ydev[d])

    def yarrive(s):
        for h in range(2):
            for d in range(2):
                if s < 3 or h == d:
                    block = sub(y - 1 - s, h) if d == 0 else sub(y + 1 + s, h)
                    arrive(block, sy.at[d, s, h], ry.at[d, s, h])
                    if s + 1 < 3 or (s + 1 == 3 and h == d):
                        ysend(s + 1, h, d)
                    send(block, block, sb.at[d, s, h], rb.at[d, s, h], sib)

    for h in range(2):
        for d in range(2):
            ysend(0, h, d)
        send(sub(y, h), sub(y, h), sb.at[2, 0, h], rb.at[2, 0, h], sib)
    for p in range(PARTS):
        for k in (1, 2):
            c = owner(0, k)
            arrive(part(c, p), sz.at[k - 1, p], rz.at[k - 1, p])
            for d in range(2):
                send(part(c, p), part(c, p), sx.at[d, k, p], rx.at[d, k, p], xdev[d])
        yarrive(p)
        for k in (1, 2):
            relay(k, p)
    yarrive(3)
    for k in range(3):
        for p in range(PARTS):
            c = owner(2, k)
            arrive(half(c, p, 0), sx.at[2, k, p], rx.at[2, k, p])
            arrive(half(c, p, 1), sx.at[3, k, p], rx.at[3, k, p])
    for h in range(2):
        arrive(rows_of(y, h, 1 - core), sb.at[2, 0, h], rb.at[2, 0, h])
        for s in range(4):
            for d in range(2):
                if s < 3 or h == d:
                    y_ = y - 1 - s if d == 0 else y + 1 + s
                    arrive(rows_of(y_, h, 1 - core), sb.at[d, s, h], rb.at[d, s, h])
    for copy in started:
        copy.wait_send()

    def fold(at):
        return at - 192 * sum((at >= 192 * n).astype(jnp.int32) for n in (1, 2, 3))

    col, row = fold(iota((128, WIDE), 1)), iota((128, WIDE), 0)
    expand = jnp.where((col >= 16 * row) & (col < 16 * row + 16), 1.0, 0.0).astype(bf16)
    row, col = fold(iota((WIDE, 128), 0)), iota((WIDE, 128), 1)
    gather = jnp.where((row >= 16 * col) & (row < 16 * col + 16), 1.0, 0.0).astype(bf16)
    at = iota((128, 128), 0)
    for j in range(8):
        rows = jnp.zeros((128, 128), f32)
        for h in range(HEADS):
            rows = jnp.where(at == h, kt_all[h, j : j + 1, :], rows)
        high, low = split(rows)
        kq[0, :, 128 * j : 128 * j + 128] = high
        kq[1, :, 128 * j : 128 * j + 128] = low

    grads = go[...]
    all_grad = dot(grads, w_all[WIDE:, :], 1, 1).astype(bf16).astype(f32)
    my_grad = dot(grads, head_o[...], 1, 1).astype(bf16).astype(f32)

    def rows_at(i):
        return pl.ds(pl.multiple_of(i * TOK, 32), TOK)

    def first(i, total):
        t = tok_all[rows_at(i), :]
        v = dot(t, w_all[:WIDE, :], 1, 1).astype(bf16)
        val[rows_at(i), :] = v
        s = dot(t, kq[0], 1, 1) + dot(t, kq[1], 1, 1)
        th = jnp.tanh(s / 8.0 / CAP)
        ex = jnp.exp(CAP * th)
        th_s[i] = th
        hp_s[i] = ex
        high, low = split(v.astype(f32) * all_grad)
        pg_s[i] = dot(high, gather, 1, 0) + dot(low, gather, 1, 0)
        return total + ex

    total = lax.fori_loop(0, CH, first, jnp.zeros((TOK, 128), f32))

    def second(i, carry):
        attended, mean = carry
        hp = hp_s[i] / total
        hp_s[i] = hp
        wide = dot(hp.astype(bf16), expand, 1, 0)
        return attended + wide * val[rows_at(i), :].astype(f32), mean + hp * pg_s[i]

    attended, mean = lax.fori_loop(
        0, CH, second, (jnp.zeros((TOK, WIDE), f32), jnp.zeros((TOK, 128), f32))
    )
    layer[...] = dot(attended.astype(bf16), w_all[WIDE:, :], 1, 0).astype(bf16)

    mine_only = lane == ch

    def third(i, my_attended):
        hp, th = hp_s[i], th_s[i]
        raw = hp * (pg_s[i] - mean) * (1.0 - th * th) / 8.0
        pg_s[i] = raw
        weight = jnp.sum(
            jnp.where(mine_only, hp.astype(bf16).astype(f32), 0.0), 1, keepdims=True
        )
        high, low = split(jnp.sum(jnp.where(mine_only, raw, 0.0), 1, keepdims=True))
        rows = weight * my_grad
        rows = jnp.where(lane == HD, high.astype(f32), rows)
        rows = jnp.where(lane == HD + 1, low.astype(f32), rows)
        left[rows_at(i), :] = rows.astype(bf16)
        v = dot(tok_all[rows_at(i), :], head_v[...], 1, 1).astype(bf16)
        return my_attended + weight * v.astype(f32)

    my_attended = lax.fori_loop(0, CH, third, jnp.zeros((TOK, 128), f32))

    hp, raw = hp_s[ch], pg_s[ch]
    wide = dot(hp.astype(bf16), expand, 1, 0)
    high, low = split(raw)
    token_grad = (
        dot((wide * all_grad).astype(bf16), w_all[:WIDE, :], 1, 0)
        + dot(high, kq[0], 1, 0)
        + dot(high, kq[1], 1, 0)
        + dot(low, kq[0], 1, 0)
    )
    mix = jnp.zeros((TOK, 128), f32)
    for c in range(CHANNELS):
        s = jnp.sum(token_grad * emb[c].astype(f32), 1, keepdims=True)
        mix = jnp.where(lane == c, s, mix)
    agg_raw = (
        agg_weight
        * (mix - jnp.sum(agg_weight * mix, 1, keepdims=True))
        * (1.0 - (capped / CAP) * (capped / CAP))
    )

    def put(i, rows):
        for c in range(2):
            g[c, i, :, :512] = rows[:, 512 * c : 512 * c + 512].astype(bf16)

    for i in range(OWN):
        g[0, i, :, 512:] = jnp.zeros((8, 128), bf16)
        g[1, i, :, 512:] = jnp.zeros((8, 128), bf16)

    def put_small(i, row):
        g[0, i, :, 512:] = stacked(row).astype(bf16)

    upright = dot(eye, pixels, 1, 1)
    one = jnp.where(iota((16, TOK), 0) == 0, 1.0, 0.0)
    grad_agg = jnp.zeros((TOK, D), f32)
    for c in range(CHANNELS):
        e = (agg_round[:, c : c + 1] * token_grad + agg_raw[:, c : c + 1] * query).astype(bf16)
        grad_agg += agg_raw[:, c : c + 1] * emb[c].astype(f32)
        rows = jnp.concatenate([upright[PP * c : PP * c + PP], one], 0).astype(bf16)
        res = dot(rows, e, 1, 0)
        put(2 * c, res[:8])
        put(2 * c + 1, res[8:16])
        put_small(c, res[16:17])
    put_small(8, jnp.sum(grad_agg, 0, keepdims=True))

    of_tokens = dot(left[...], tok_all[...], 0, 0)
    of_grads = dot(my_attended.astype(bf16), grads, 0, 0)
    for i in range(8):
        put(16 + i, of_tokens[8 * i : 8 * i + 8])
        put(24 + i, of_grads[8 * i : 8 * i + 8])
    put_small(9, of_tokens[HD : HD + 1] + of_tokens[HD + 1 : HD + 2])

    pair = remote(g.at[1 - core], half_in, s0, r0, sib)
    pair.start()
    pair.wait_recv()
    acc[...] = (g[core].astype(f32) + half_in[...].astype(f32)).astype(bf16)

    @pl.loop(1, OWN)
    def _(j):
        to = (own + j) % OWN
        remote(acc.at[to], held.at[own], s1.at[to], r1.at[own], (to * 2 + core, ch)).start()

    def add(j, total):
        at = (own + OWN - j) % OWN
        remote(acc.at[at], held.at[at], s1.at[at], r1.at[at], sib).wait_recv()
        return total + held[at].astype(f32)

    mine[...] = lax.fori_loop(1, OWN, add, acc[own].astype(f32)).astype(bf16)

    @pl.loop(1, OWN)
    def _(j):
        to = (own + j) % OWN
        remote(mine, out.at[core, own], s2.at[to], r2.at[own], (to * 2 + core, ch)).start()

    out[core, own] = mine[...]

    @pl.loop(1, OWN)
    def _(j):
        at = (own + OWN - j) % OWN
        remote(mine, out.at[core, at], s2.at[at], r2.at[at], sib).wait_recv()

    back = remote(out.at[core], out.at[core], s3, r3, sib)
    back.start()
    remote(out.at[1 - core], out.at[1 - core], s3, r3, sib).wait_recv()
    back.wait_send()
    pair.wait_send()

    @pl.loop(1, OWN)
    def _(j):
        to = (own + j) % OWN
        remote(acc.at[to], held.at[own], s1.at[to], r1.at[own], sib).wait_send()
        remote(mine, out.at[core, own], s2.at[to], r2.at[own], sib).wait_send()


def step(*args):
    vmem = pl.BlockSpec(memory_space=pltpu.VMEM)
    dma = pltpu.SemaphoreType.DMA
    shape = (OWN, 8, LANES)
    return pl.pallas_call(
        step_kernel,
        out_shape=(
            jax.ShapeDtypeStruct((TOK, D), bf16),
            jax.ShapeDtypeStruct((2, *shape), bf16),
        ),
        in_specs=[vmem] * len(args),
        out_specs=(vmem, vmem),
        scratch_shapes=[
            pltpu.VMEM((CHANNELS, TOK, D), bf16),
            pltpu.VMEM((CH * TOK, D), bf16),
            pltpu.VMEM((NY * CH * 16, D), bf16),
            pltpu.VMEM((CH, 8, 128), f32),
            pltpu.VMEM((TOK, D), bf16),
            pltpu.VMEM((NY, 16, D), bf16),
            pltpu.VMEM((8, 128), f32),
            pltpu.VMEM((128, D), bf16),
            pltpu.VMEM((128, D), bf16),
            pltpu.VMEM((2, 128, D), bf16),
            pltpu.VMEM((CH * TOK, WIDE), bf16),
            pltpu.VMEM((CH * TOK, 128), bf16),
            pltpu.VMEM((CH, TOK, 128), f32),
            pltpu.VMEM((CH, TOK, 128), f32),
            pltpu.VMEM((CH, TOK, 128), f32),
            pltpu.VMEM((2, *shape), bf16),
            pltpu.VMEM(shape, bf16),
            pltpu.VMEM(shape, bf16),
            pltpu.VMEM(shape[1:], bf16),
            pltpu.VMEM(shape, bf16),
            dma((2, PARTS)),
            dma((2, PARTS)),
            dma((4, 3, PARTS)),
            dma((4, 3, PARTS)),
            dma((2, 11)),
            dma((2, 11)),
            dma((2, 4, 2)),
            dma((2, 4, 2)),
            dma((3, 4, 2)),
            dma((3, 4, 2)),
            dma,
            dma,
            dma((OWN,)),
            dma((OWN,)),
            dma((OWN,)),
            dma((OWN,)),
            dma,
            dma,
            dma,
        ],
        compiler_params=pltpu.CompilerParams(collective_id=0, has_side_effects=True),
        name="step",
    )(*args)


def finish_kernel(g, fq, kw, embed, bias, agg, key, value, query, outg):
    eye = (iota((HD, HD), 0) == iota((HD, HD), 1)).astype(f32).astype(bf16)

    def rows(i):
        return jnp.concatenate([g[0, i, :, :512], g[1, i, :, :512]], 1)

    def row(i):
        block = g[0, i, :, 512:].astype(f32)
        return jnp.concatenate([block[j : j + 1] for j in range(8)], 1)

    for i in range(16):
        embed[8 * i : 8 * i + 8, :] = rows(i).astype(f32)
    for i in range(8):
        bias[i : i + 1, :] = row(i)
        outg[8 * i : 8 * i + 8, :] = rows(24 + i).astype(f32)
        value_rows = rows(16 + i).astype(f32).astype(bf16)
        part = dot(value_rows, eye[8 * i : 8 * i + 8], 0, 0)
        total = part if i == 0 else total + part
    value[...] = total
    agg[...] = row(8)
    u = row(9)
    u_rows = jnp.broadcast_to(u, (16, D)).astype(bf16)
    only = jnp.where(iota((16, HD), 0) == 0, fq[...].astype(f32), 0.0).astype(bf16)
    key[...] = dot(u_rows, only, 0, 0)
    query[...] = dot(u_rows, kw[...], 1, 0)[:1]


def finish(summed, final_query, key_weight):
    vmem = pl.BlockSpec(memory_space=pltpu.VMEM)

    def shape(*dims):
        return jax.ShapeDtypeStruct(dims, f32)

    return pl.pallas_call(
        finish_kernel,
        out_shape=(
            shape(CHANNELS * PP, D),
            shape(CHANNELS, D),
            shape(1, D),
            shape(D, HD),
            shape(D, HD),
            shape(1, HD),
            shape(HD, D),
        ),
        in_specs=[vmem] * 3,
        out_specs=(vmem,) * 7,
        name="finish",
    )(summed, final_query, key_weight)


def per_device(
    pixels,
    embed_weight,
    channel_bias,
    agg_query,
    key_weight,
    value_weight,
    final_query,
    out_weight,
    group_counts,
    grad_output,
):
    layer_out, summed = step(
        pixels,
        embed_weight.reshape(CHANNELS * PP, D),
        channel_bias,
        agg_query,
        key_weight,
        value_weight,
        final_query,
        out_weight,
        group_counts.reshape(1, 1),
        grad_output,
    )
    embed, bias, agg, key, value, query, outg = finish(summed, final_query, key_weight)
    return layer_out, embed.reshape(CHANNELS, PP, D), bias, agg, key, value, query, outg


def solution(mesh):
    in_specs = (
        P("dp", "chan"),
        P("chan", None, None),
        P("chan", None),
        P("chan", None),
        P(None, "chan"),
        P(None, "chan"),
        P("chan", None),
        P("chan", None),
        P("chan"),
        P("dp", None),
    )
    out_specs = (
        P("dp", None),
        P("chan", None, None),
        P("chan", None),
        P("chan", None),
        P(None, "chan"),
        P(None, "chan"),
        P("chan", None),
        P("chan", None),
    )
    return jax.shard_map(
        per_device, mesh=mesh, in_specs=in_specs, out_specs=out_specs, check_vma=False
    )
```

time: 166 us -> 122 us (0.73)
  matrix products: 25.8 us -> 0 us
  other arithmetic: 15.9 us -> 0 us
  local copies, waits for them, and re-layouts: 20.2 us -> 6.22 us
  Pallas kernels: 101 us -> 114 us
    dot_general x19 -> x0, matrix products: 25.8 us -> none  [the longest x13 19.1 us: dot(): lax.dot_general(a, b, (((ca,), (cb,)), ((), ())), preferred_element_type=...]
    pallas_call x2, Pallas kernels: 101 us -> 114 us  [the longest x1 111 us: step(): pl.pallas_call(step_kernel, out_shape=(jax.ShapeDtypeStruct((TOK, D), bf1...]
    reduce_sum x7 -> x0, other arithmetic: 5.28 us -> none  [the longest x1 2.32 us: per_device(): jnp.sum((spread * values.astype(f32)).reshape(CH, TOK, HEADS * HD), 0)]
    convert_element_type x11 -> x0, other arithmetic: 3.72 us -> none  [the longest x1 1.18 us: per_device(): summed = sum_over_dp(packed).astype(f32)]
    concatenate x4 -> x0, other arithmetic: 2.82 us -> none  [the longest x1 1.38 us: per_device(): shard = jnp.concatenate([value_weight.T, out_weight], 0)]
    reshape x5 -> x0, local copies, waits for them, and re-layouts: 2.71 us -> none  [the longest x1 0.98 us: per_device(): (dot(high, expand, 1, 1) + dot(low, expand, 1, 1)).reshape(CH, TOK, HEADS)]
    slice x5 -> x0, local copies, waits for them, and re-layouts: 2.68 us -> none  [the longest x1 1.27 us: per_device(): few[8:9]]
    convert_element_type x5 -> x0, local copies, waits for them, and re-layouts: 2.38 us -> none  [the longest x2 1.15 us: split(): return (high.astype(bf16), (value - high).astype(bf16))]
where the time goes in v2:
time: 122 us
  Pallas kernels  114 us (93%)
  local copies, waits for them, and re-layouts  6.22 us (5%)
  between operations  1.3 us (1%)
    pallas_call x1, Pallas kernels, step(): pl.pallas_call(step_kernel, out_shape=(jax.ShapeDtypeStruct((TOK, D), bf1...  111 us
    unnamed x11, local copies, waits for them, and re-layouts  6.22 us
    pallas_call x1, Pallas kernels, finish(): pl.pallas_call(finish_kernel, out_shape=(shape(CHANNELS * PP, D), shape(C...  3.21 us

profile of v2, /device:TPU:1, one launch (start us, length us, event | category | flops | bytes accessed | tf_op | source)
XLA Modules:
  0.0 121.5 jit_solution(869396152688831276)
XLA Ops:
  1.3 0.0 copy-start.2
  1.3 1.8 %copy.18.kw = bf16[1024,64]{1,0:T(8,128)(2,1)} copy(bf16[1024,64]{0,1:T(8,128)(2,1)} %param.14) | data formatting | bytes 262144 | tf_op args[4]
  3.1 0.0 copy-done.2
  3.1 0.8 copy.19.vw
  3.9 110.8 %step.1 = (bf16[96,1024]{1,0:T(8,128)(2,1)}, bf16[2,32,8,640]{3,2,1,0:T(8,128)(2,1)}) custom-call(bf16[96,128]{1,0:T(8,128)(2,1)} %pix.1, bf16[128,1024]{1,0:T(8,128)(2,1)} %bitcast.4, bf16[8,1024]{1,0:T(8,128)(2,1)} %bias.1, bf16[1,1024]{1,0:T(2,128)(2,1)} %aggq.1, bf16[1024,64]{1,0:T(8,128)(2,1)} %copy.18.kw, bf16[1024,64]{1,0:T(8,128)(2,1)} %copy.19.vw, ...), custom_call_target="tpu_custom_call" | custom-call | tf_op jit(solution)/shard_map/step/pallas_call | solution.py:459
  114.7 3.2 %finish.1 = (f32[128,1024]{1,0:T(8,128)}, f32[8,1024]{1,0:T(8,128)}, f32[1,1024]{1,0:T(1,128)}, f32[1024,64]{1,0:T(8,128)}, f32[1024,64]{1,0:T(8,128)}, /*index=5*/f32[1,64]{1,0:T(1,128)}, f32[64,1024]{1,0:T(8,128)}) custom-call(bf16[2,32,8,640]{3,2,1,0:T(8,128)(2,1)} %get-tuple-element.18.g, bf16[1,64]{1,0:T(2,128)(2,1)} %fq.3, bf16[1024,64]{1,0:T(8,128)(2,1)} %copy.18.kw), custom_call_target="tpu_custom_call" | custom-call | tf_op jit(solution)/shard_map/finish/pallas_call | solution.py:546
  117.9 0.0 copy-start
  117.9 2.0 %copy.21 = f32[1024,64]{0,1:T(8,128)} copy(f32[1024,64]{1,0:T(8,128)} %get-tuple-element.30) | data formatting | bytes 524288
  119.9 0.0 copy-done
  119.9 0.0 copy-start.1
  119.9 0.9 copy.22
  120.8 0.0 copy-done.1
  120.8 0.7 copy.25
Async XLA Ops:
  1.3 1.8 %copy-start.2 = (bf16[1024,64]{0,1:T(8,128)(2,1)S(1)}, bf16[1024,64]{0,1:T(8,128)(2,1)}, u32[]{:S(2)}) copy-start(bf16[1024,64]{0,1:T(8,128)(2,1)} %param.15) | copy-start | bytes 393220
  117.9 2.0 %copy-start = (f32[1024,64]{1,0:T(8,128)S(1)}, f32[1024,64]{1,0:T(8,128)}, u32[]{:S(2)}) copy-start(f32[1024,64]{1,0:T(8,128)} %get-tuple-element.31) | copy-start | bytes 786436
  119.9 0.9 copy-start.1

commit v3 on v2

--- a/solution.py
+++ b/solution.py
@@ -16,8 +16,10 @@
 PR = TOK // PARTS
 PH = PR // 2
 CAP = 15.0
-LANES = 640
 OWN = NY * NL
+FEW = 5
+BATCH = 4
+ROWS = BATCH * TOK
 
 f32, bf16 = jnp.float32, jnp.bfloat16
 
@@ -55,7 +57,9 @@
     counts,
     go,
     layer,
-    out,
+    out_a,
+    out_b,
+    out_c,
     emb,
     tok_all,
     w_all,
@@ -63,7 +67,6 @@
     tok,
     wp,
     kt,
-    head_v,
     head_o,
     kq,
     val,
@@ -71,11 +74,22 @@
     th_s,
     hp_s,
     pg_s,
-    g,
-    half_in,
-    held,
-    mine,
-    acc,
+    mv_s,
+    g_a,
+    g_b,
+    g_c,
+    half_a,
+    half_b,
+    half_c,
+    held_a,
+    held_b,
+    held_c,
+    mine_a,
+    mine_b,
+    mine_c,
+    acc_a,
+    acc_b,
+    acc_c,
     sz,
     rz,
     sx,
@@ -145,16 +159,15 @@
     tok_all[pl.ds(pl.multiple_of(ch * TOK, 32), TOK), :] = tok[...]
 
     eye = (iota((128, 128), 0) == iota((128, 128), 1)).astype(f32).astype(bf16)
-    flipped = dot(eye[:HD, :HD], vw[...], 1, 1)
-    head_v[:HD] = flipped.astype(bf16)
-    head_v[HD:] = jnp.zeros((HD, D), bf16)
+    kq[256 : 256 + HD] = vw[...]
+    kq[256 + HD :] = jnp.zeros((HD, D), bf16)
     head_o[:HD] = outw[...]
     head_o[HD:] = jnp.zeros((HD, D), bf16)
     for q in range(4):
-        wp[q] = head_v[16 * q : 16 * q + 16, :]
+        wp[q] = vw[16 * q : 16 * q + 16, :]
         wp[4 + q] = outw[16 * q : 16 * q + 16, :]
     fq8 = jnp.broadcast_to(fq[...].astype(f32), (16, HD)).astype(bf16)
-    kt[...] = stacked(dot(fq8, kw[...], 1, 1)[:1])
+    kt[...] = stacked(dot(fq8, kw[...], 1, 0)[:1])
     kt_all[ch] = kt[...]
 
     started = []
@@ -304,70 +317,106 @@
         for h in range(HEADS):
             rows = jnp.where(at == h, kt_all[h, j : j + 1, :], rows)
         high, low = split(rows)
-        kq[0, :, 128 * j : 128 * j + 128] = high
-        kq[1, :, 128 * j : 128 * j + 128] = low
+        kq[:128, 128 * j : 128 * j + 128] = high
+        kq[128:256, 128 * j : 128 * j + 128] = low
 
     grads = go[...]
     all_grad = dot(grads, w_all[WIDE:, :], 1, 1).astype(bf16).astype(f32)
     my_grad = dot(grads, head_o[...], 1, 1).astype(bf16).astype(f32)
 
     def rows_at(i):
-        return pl.ds(pl.multiple_of(i * TOK, 32), TOK)
+        return pl.ds(pl.multiple_of(i * ROWS, 128), ROWS)
+
+    def folded(value):
+        return jnp.sum(value.reshape(BATCH, TOK, value.shape[1]), 0)
+
+    def tiled(value):
+        return jnp.concatenate([value] * BATCH, 0)
+
+    all_tiled = tiled(all_grad)
 
     def first(i, total):
         t = tok_all[rows_at(i), :]
         v = dot(t, w_all[:WIDE, :], 1, 1).astype(bf16)
         val[rows_at(i), :] = v
-        s = dot(t, kq[0], 1, 1) + dot(t, kq[1], 1, 1)
-        th = jnp.tanh(s / 8.0 / CAP)
+        high, low = split(v.astype(f32) * all_tiled)
+        pg_s[rows_at(i), :] = dot(high, gather, 1, 0) + dot(low, gather, 1, 0)
+        r = dot(t, kq[...], 1, 1)
+        th = jnp.tanh((r[:, :128] + r[:, 128:256]) / 8.0 / CAP)
         ex = jnp.exp(CAP * th)
-        th_s[i] = th
-        hp_s[i] = ex
-        high, low = split(v.astype(f32) * all_grad)
-        pg_s[i] = dot(high, gather, 1, 0) + dot(low, gather, 1, 0)
-        return total + ex
-
-    total = lax.fori_loop(0, CH, first, jnp.zeros((TOK, 128), f32))
+        th_s[rows_at(i), :] = th
+        hp_s[rows_at(i), :] = ex
+        mv_s[rows_at(i), :] = r[:, 256:].astype(bf16)
+        return total + folded(ex)
+
+    total = lax.fori_loop(0, CH // BATCH, first, jnp.zeros((TOK, 128), f32))
+    inverse = tiled(1.0 / total)
 
     def second(i, carry):
         attended, mean = carry
-        hp = hp_s[i] / total
-        hp_s[i] = hp
+        hp = hp_s[rows_at(i), :] * inverse
+        hp_s[rows_at(i), :] = hp
         wide = dot(hp.astype(bf16), expand, 1, 0)
-        return attended + wide * val[rows_at(i), :].astype(f32), mean + hp * pg_s[i]
+        return (
+            attended + folded(wide * val[rows_at(i), :].astype(f32)),
+            mean + folded(hp * pg_s[rows_at(i), :]),
+        )
 
     attended, mean = lax.fori_loop(
-        0, CH, second, (jnp.zeros((TOK, WIDE), f32), jnp.zeros((TOK, 128), f32))
+        0, CH // BATCH, second, (jnp.zeros((TOK, WIDE), f32), jnp.zeros((TOK, 128), f32))
     )
     layer[...] = dot(attended.astype(bf16), w_all[WIDE:, :], 1, 0).astype(bf16)
 
-    mine_only = lane == ch
+    lane_tiled = iota((ROWS, 128), 1)
+    mine_only = lane_tiled == ch
+    mean_tiled, my_tiled = tiled(mean), tiled(my_grad)
 
     def third(i, my_attended):
-        hp, th = hp_s[i], th_s[i]
-        raw = hp * (pg_s[i] - mean) * (1.0 - th * th) / 8.0
-        pg_s[i] = raw
+        hp, th = hp_s[rows_at(i), :], th_s[rows_at(i), :]
+        raw = hp * (pg_s[rows_at(i), :] - mean_tiled) * (1.0 - th * th) / 8.0
+        pg_s[rows_at(i), :] = raw
         weight = jnp.sum(
             jnp.where(mine_only, hp.astype(bf16).astype(f32), 0.0), 1, keepdims=True
         )
         high, low = split(jnp.sum(jnp.where(mine_only, raw, 0.0), 1, keepdims=True))
-        rows = weight * my_grad
-        rows = jnp.where(lane == HD, high.astype(f32), rows)
-        rows = jnp.where(lane == HD + 1, low.astype(f32), rows)
+        rows = weight * my_tiled
+        rows = jnp.where(lane_tiled == HD, high.astype(f32), rows)
+        rows = jnp.where(lane_tiled == HD + 1, low.astype(f32), rows)
         left[rows_at(i), :] = rows.astype(bf16)
-        v = dot(tok_all[rows_at(i), :], head_v[...], 1, 1).astype(bf16)
-        return my_attended + weight * v.astype(f32)
-
-    my_attended = lax.fori_loop(0, CH, third, jnp.zeros((TOK, 128), f32))
-
-    hp, raw = hp_s[ch], pg_s[ch]
+        return my_attended + folded(weight * mv_s[rows_at(i), :].astype(f32))
+
+    my_attended = lax.fori_loop(0, CH // BATCH, third, jnp.zeros((TOK, 128), f32))
+
+    def put(ref, i, rows):
+        for c in range(2):
+            for q in range(2):
+                at = 512 * c + 256 * q
+                ref[c, 2 * i + q] = rows[:, at : at + 256].astype(bf16)
+
+    def put_small(i, row):
+        g_c[i // FEW, i % FEW] = stacked(row).astype(bf16)
+
+    of_tokens = dot(left[...], tok_all[...], 0, 0)
+    put_small(9, of_tokens[HD : HD + 1] + of_tokens[HD + 1 : HD + 2])
+    of_grads = dot(my_attended.astype(bf16), grads, 0, 0)
+    for i in range(8):
+        put(g_a, i, of_tokens[8 * i : 8 * i + 8])
+        put(g_a, 8 + i, of_grads[8 * i : 8 * i + 8])
+
+    def pair(ref, half, n):
+        return remote(ref.at[1 - core], half, s0.at[n], r0.at[n], sib)
+
+    pair(g_a, half_a, 0).start()
+
+    here = pl.ds(pl.multiple_of(ch * TOK, 32), TOK)
+    hp, raw = hp_s[here, :], pg_s[here, :]
     wide = dot(hp.astype(bf16), expand, 1, 0)
     high, low = split(raw)
     token_grad = (
         dot((wide * all_grad).astype(bf16), w_all[:WIDE, :], 1, 0)
-        + dot(high, kq[0], 1, 0)
-        + dot(high, kq[1], 1, 0)
-        + dot(low, kq[0], 1, 0)
+        + dot(high, kq[:128], 1, 0)
+        + dot(high, kq[128:256], 1, 0)
+        + dot(low, kq[:128], 1, 0)
     )
     mix = jnp.zeros((TOK, 128), f32)
     for c in range(CHANNELS):
@@ -379,16 +428,37 @@
         * (1.0 - (capped / CAP) * (capped / CAP))
     )
 
-    def put(i, rows):
-        for c in range(2):
-            g[c, i, :, :512] = rows[:, 512 * c : 512 * c + 512].astype(bf16)
-
-    for i in range(OWN):
-        g[0, i, :, 512:] = jnp.zeros((8, 128), bf16)
-        g[1, i, :, 512:] = jnp.zeros((8, 128), bf16)
-
-    def put_small(i, row):
-        g[0, i, :, 512:] = stacked(row).astype(bf16)
+    def pair_sum(ref, half, acc, n):
+        pair(ref, half, n).wait_recv()
+        acc[...] = (ref[core].astype(f32) + half[...].astype(f32)).astype(bf16)
+
+    def peer(j):
+        return (j * 2 + core, ch)
+
+    def spread_out(acc, held, n):
+        @pl.loop(1, OWN)
+        def _(j):
+            to = (own + j) % OWN
+            remote(acc.at[to], held.at[own], s1.at[n, to], r1.at[n, own], peer(to)).start()
+
+    def total_of(acc, held, at, n):
+        def add(j, total):
+            src = (own + OWN - j) % OWN
+            remote(held.at[src], held.at[src], s1.at[n, src], r1.at[n, src], sib).wait_recv()
+            return total + held[src].astype(f32)
+
+        return lax.fori_loop(1, OWN, add, acc[at].astype(f32)).astype(bf16)
+
+    def give(mine, out, n):
+        @pl.loop(1, OWN)
+        def _(j):
+            to = (own + j) % OWN
+            remote(mine, out.at[core, own], s2.at[n, to], r2.at[n, own], peer(to)).start()
+
+        out[core, own] = mine[...]
+
+    pair_sum(g_a, half_a, acc_a, 0)
+    spread_out(acc_a, held_a, 0)
 
     upright = dot(eye, pixels, 1, 1)
     one = jnp.where(iota((16, TOK), 0) == 0, 1.0, 0.0)
@@ -398,72 +468,98 @@
         grad_agg += agg_raw[:, c : c + 1] * emb[c].astype(f32)
         rows = jnp.concatenate([upright[PP * c : PP * c + PP], one], 0).astype(bf16)
         res = dot(rows, e, 1, 0)
-        put(2 * c, res[:8])
-        put(2 * c + 1, res[8:16])
         put_small(c, res[16:17])
+        put(g_b, 2 * c, res[:8])
+        put(g_b, 2 * c + 1, res[8:16])
+    pair(g_b, half_b, 1).start()
     put_small(8, jnp.sum(grad_agg, 0, keepdims=True))
 
-    of_tokens = dot(left[...], tok_all[...], 0, 0)
-    of_grads = dot(my_attended.astype(bf16), grads, 0, 0)
-    for i in range(8):
-        put(16 + i, of_tokens[8 * i : 8 * i + 8])
-        put(24 + i, of_grads[8 * i : 8 * i + 8])
-    put_small(9, of_tokens[HD : HD + 1] + of_tokens[HD + 1 : HD + 2])
-
-    pair = remote(g.at[1 - core], half_in, s0, r0, sib)
-    pair.start()
-    pair.wait_recv()
-    acc[...] = (g[core].astype(f32) + half_in[...].astype(f32)).astype(bf16)
-
-    @pl.loop(1, OWN)
-    def _(j):
-        to = (own + j) % OWN
-        remote(acc.at[to], held.at[own], s1.at[to], r1.at[own], (to * 2 + core, ch)).start()
-
-    def add(j, total):
-        at = (own + OWN - j) % OWN
-        remote(acc.at[at], held.at[at], s1.at[at], r1.at[at], sib).wait_recv()
-        return total + held[at].astype(f32)
-
-    mine[...] = lax.fori_loop(1, OWN, add, acc[own].astype(f32)).astype(bf16)
-
-    @pl.loop(1, OWN)
-    def _(j):
-        to = (own + j) % OWN
-        remote(mine, out.at[core, own], s2.at[to], r2.at[own], (to * 2 + core, ch)).start()
-
-    out[core, own] = mine[...]
-
-    @pl.loop(1, OWN)
-    def _(j):
-        at = (own + OWN - j) % OWN
-        remote(mine, out.at[core, at], s2.at[at], r2.at[at], sib).wait_recv()
-
-    back = remote(out.at[core], out.at[core], s3, r3, sib)
-    back.start()
-    remote(out.at[1 - core], out.at[1 - core], s3, r3, sib).wait_recv()
-    back.wait_send()
-    pair.wait_send()
-
-    @pl.loop(1, OWN)
-    def _(j):
-        to = (own + j) % OWN
-        remote(acc.at[to], held.at[own], s1.at[to], r1.at[own], sib).wait_send()
-        remote(mine, out.at[core, own], s2.at[to], r2.at[own], sib).wait_send()
+    pair_sum(g_b, half_b, acc_b, 1)
+    pair(g_c, half_c, 2).start()
+    spread_out(acc_b, held_b, 1)
+    pair_sum(g_c, half_c, acc_c, 2)
+    for i in range(FEW):
+
+        @pl.when(own != i)
+        def _():
+            remote(acc_c.at[i], held_c.at[own], s1.at[2, i], r1.at[2, own], peer(i)).start()
+
+    mine_a[...] = total_of(acc_a, held_a, own, 0)
+    give(mine_a, out_a, 0)
+    mine_b[...] = total_of(acc_b, held_b, own, 1)
+    give(mine_b, out_b, 1)
+
+    @pl.when(own < FEW)
+    def _():
+        mine_c[...] = total_of(acc_c, held_c, own, 2)
+        give(mine_c, out_c, 2)
+
+    def taken(out, n):
+        @pl.loop(1, OWN)
+        def _(j):
+            src = (own + OWN - j) % OWN
+            block = out.at[core, src]
+            remote(block, block, s2.at[n, src], r2.at[n, src], sib).wait_recv()
+
+    def back(out, n):
+        return remote(out.at[core], out.at[core], s3.at[n], r3.at[n], sib)
+
+    taken(out_a, 0)
+    back(out_a, 0).start()
+    taken(out_b, 1)
+    back(out_b, 1).start()
+    for i in range(FEW):
+
+        @pl.when(own != i)
+        def _():
+            block = out_c.at[core, i]
+            remote(block, block, s2.at[2, i], r2.at[2, i], sib).wait_recv()
+
+    back(out_c, 2).start()
+    for n, out in enumerate((out_a, out_b, out_c)):
+        other = out.at[1 - core]
+        remote(other, other, s3.at[n], r3.at[n], sib).wait_recv()
+        back(out, n).wait_send()
+    for n, (ref, half) in enumerate(((g_a, half_a), (g_b, half_b), (g_c, half_c))):
+        pair(ref, half, n).wait_send()
+
+    def sent(acc, held, mine, out, n):
+        @pl.loop(1, OWN)
+        def _(j):
+            to = (own + j) % OWN
+            remote(acc.at[to], held.at[own], s1.at[n, to], r1.at[n, own], sib).wait_send()
+            remote(mine, out.at[core, own], s2.at[n, to], r2.at[n, own], sib).wait_send()
+
+    sent(acc_a, held_a, mine_a, out_a, 0)
+    sent(acc_b, held_b, mine_b, out_b, 1)
+    for i in range(FEW):
+
+        @pl.when(own != i)
+        def _():
+            remote(acc_c.at[i], held_c.at[own], s1.at[2, i], r1.at[2, own], sib).wait_send()
+
+    @pl.when(own < FEW)
+    def _():
+        @pl.loop(1, OWN)
+        def _(j):
+            to = (own + j) % OWN
+            remote(mine_c, out_c.at[core, own], s2.at[2, to], r2.at[2, own], sib).wait_send()
 
 
 def step(*args):
     vmem = pl.BlockSpec(memory_space=pltpu.VMEM)
     dma = pltpu.SemaphoreType.DMA
-    shape = (OWN, 8, LANES)
+    large, few = (OWN, 8, 256), (FEW, 8, 128)
     return pl.pallas_call(
         step_kernel,
         out_shape=(
             jax.ShapeDtypeStruct((TOK, D), bf16),
-            jax.ShapeDtypeStruct((2, *shape), bf16),
+            jax.ShapeDtypeStruct((2, *large), bf16),
+            jax.ShapeDtypeStruct((2, *large), bf16),
+            jax.ShapeDtypeStruct((2, *few), bf16),
         ),
         in_specs=[vmem] * len(args),
-        out_specs=(vmem, vmem),
+        out_specs=(vmem,) * 4,
         scratch_shapes=[
             pltpu.VMEM((CHANNELS, TOK, D), bf16),
             pltpu.VMEM((CH * TOK, D), bf16),
@@ -473,18 +569,28 @@
             pltpu.VMEM((NY, 16, D), bf16),
             pltpu.VMEM((8, 128), f32),
             pltpu.VMEM((128, D), bf16),
-            pltpu.VMEM((128, D), bf16),
-            pltpu.VMEM((2, 128, D), bf16),
+            pltpu.VMEM((384, D), bf16),
             pltpu.VMEM((CH * TOK, WIDE), bf16),
             pltpu.VMEM((CH * TOK, 128), bf16),
-            pltpu.VMEM((CH, TOK, 128), f32),
-            pltpu.VMEM((CH, TOK, 128), f32),
-            pltpu.VMEM((CH, TOK, 128), f32),
-            pltpu.VMEM((2, *shape), bf16),
-            pltpu.VMEM(shape, bf16),
-            pltpu.VMEM(shape, bf16),
-            pltpu.VMEM(shape[1:], bf16),
-            pltpu.VMEM(shape, bf16),
+            pltpu.VMEM((CH * TOK, 128), f32),
+            pltpu.VMEM((CH * TOK, 128), f32),
+            pltpu.VMEM((CH * TOK, 128), f32),
+            pltpu.VMEM((CH * TOK, 128), bf16),
+            pltpu.VMEM((2, *large), bf16),
+            pltpu.VMEM((2, *large), bf16),
+            pltpu.VMEM((2, *few), bf16),
+            pltpu.VMEM(large, bf16),
+            pltpu.VMEM(large, bf16),
+            pltpu.VMEM(few, bf16),
+            pltpu.VMEM(large, bf16),
+            pltpu.VMEM(large, bf16),
+            pltpu.VMEM((OWN, 8, 128), bf16),
+            pltpu.VMEM(large[1:], bf16),
+            pltpu.VMEM(large[1:], bf16),
+            pltpu.VMEM(few[1:], bf16),
+            pltpu.VMEM(large, bf16),
+            pltpu.VMEM(large, bf16),
+            pltpu.VMEM(few, bf16),
             dma((2, PARTS)),
             dma((2, PARTS)),
             dma((4, 3, PARTS)),
@@ -495,14 +601,14 @@
             dma((2, 4, 2)),
             dma((3, 4, 2)),
             dma((3, 4, 2)),
-            dma,
-            dma,
-            dma((OWN,)),
-            dma((OWN,)),
-            dma((OWN,)),
-            dma((OWN,)),
-            dma,
-            dma,
+            dma((3,)),
+            dma((3,)),
+            dma((3, OWN)),
+            dma((3, OWN)),
+            dma((3, OWN)),
+            dma((3, OWN)),
+            dma((3,)),
+            dma((3,)),
             dma,
         ],
         compiler_params=pltpu.CompilerParams(collective_id=0, has_side_effects=True),
@@ -510,34 +616,30 @@
     )(*args)
 
 
-def finish_kernel(g, fq, kw, embed, bias, agg, key, value, query, outg):
-    eye = (iota((HD, HD), 0) == iota((HD, HD), 1)).astype(f32).astype(bf16)
-
-    def rows(i):
-        return jnp.concatenate([g[0, i, :, :512], g[1, i, :, :512]], 1)
+def finish_kernel(layer_in, a, b, few, fq, kw, layer, embed, bias, agg, key, value, query, outg):
+    def rows(ref, i):
+        parts = [ref[c, 2 * i + q] for c in range(2) for q in range(2)]
+        return jnp.concatenate(parts, 1).astype(f32)
 
     def row(i):
-        block = g[0, i, :, 512:].astype(f32)
+        block = few[i // FEW, i % FEW].astype(f32)
         return jnp.concatenate([block[j : j + 1] for j in range(8)], 1)
 
+    layer[...] = layer_in[...]
     for i in range(16):
-        embed[8 * i : 8 * i + 8, :] = rows(i).astype(f32)
+        embed[8 * i : 8 * i + 8, :] = rows(b, i)
     for i in range(8):
         bias[i : i + 1, :] = row(i)
-        outg[8 * i : 8 * i + 8, :] = rows(24 + i).astype(f32)
-        value_rows = rows(16 + i).astype(f32).astype(bf16)
-        part = dot(value_rows, eye[8 * i : 8 * i + 8], 0, 0)
-        total = part if i == 0 else total + part
-    value[...] = total
+        value[8 * i : 8 * i + 8, :] = rows(a, i)
+        outg[8 * i : 8 * i + 8, :] = rows(a, 8 + i)
     agg[...] = row(8)
-    u = row(9)
-    u_rows = jnp.broadcast_to(u, (16, D)).astype(bf16)
+    u_rows = jnp.broadcast_to(row(9), (16, D)).astype(bf16)
     only = jnp.where(iota((16, HD), 0) == 0, fq[...].astype(f32), 0.0).astype(bf16)
-    key[...] = dot(u_rows, only, 0, 0)
-    query[...] = dot(u_rows, kw[...], 1, 0)[:1]
-
-
-def finish(summed, final_query, key_weight):
+    key[...] = dot(only, u_rows, 0, 0)
+    query[...] = dot(u_rows, kw[...], 1, 1)[:1]
+
+
+def finish(*args):
     vmem = pl.BlockSpec(memory_space=pltpu.VMEM)
 
     def shape(*dims):
@@ -546,18 +648,19 @@
     return pl.pallas_call(
         finish_kernel,
         out_shape=(
+            jax.ShapeDtypeStruct((TOK, D), bf16),
             shape(CHANNELS * PP, D),
             shape(CHANNELS, D),
             shape(1, D),
-            shape(D, HD),
-            shape(D, HD),
+            shape(HD, D),
+            shape(HD, D),
             shape(1, HD),
             shape(HD, D),
         ),
-        in_specs=[vmem] * 3,
-        out_specs=(vmem,) * 7,
+        in_specs=[vmem] * len(args),
+        out_specs=(vmem,) * 8,
         name="finish",
-    )(summed, final_query, key_weight)
+    )(*args)
 
 
 def per_device(
@@ -572,20 +675,21 @@
     group_counts,
     grad_output,
 ):
-    layer_out, summed = step(
+    key_rows = key_weight.T
+    partial = step(
         pixels,
         embed_weight.reshape(CHANNELS * PP, D),
         channel_bias,
         agg_query,
-        key_weight,
-        value_weight,
+        key_rows,
+        value_weight.T,
         final_query,
         out_weight,
         group_counts.reshape(1, 1),
         grad_output,
     )
-    embed, bias, agg, key, value, query, outg = finish(summed, final_query, key_weight)
-    return layer_out, embed.reshape(CHANNELS, PP, D), bias, agg, key, value, query, outg
+    layer_out, embed, bias, agg, key, value, query, outg = finish(*partial, final_query, key_rows)
+    return layer_out, embed.reshape(CHANNELS, PP, D), bias, agg, key.T, value.T, query, outg
 
 
 def solution(mesh):

time: 122 us -> 106 us (0.87)
  Pallas kernels: 114 us -> 105 us
  local copies, waits for them, and re-layouts: 6.22 us -> 0 us
    pallas_call x1, Pallas kernels: 111 us -> 102 us  [step(): pl.pallas_call(step_kernel, out_shape=(jax.ShapeDtypeStruct((TOK, D), bf1...]
    unnamed x11 -> x0, local copies, waits for them, and re-layouts: 6.22 us -> none
where the time goes in v3:
time: 106 us
  Pallas kernels  105 us (99%)
  between operations  1.29 us (1%)
    pallas_call x1, Pallas kernels, step(): pl.pallas_call(step_kernel, out_shape=(jax.ShapeDtypeStruct((TOK, D), bf1...  102 us
    pallas_call x1, Pallas kernels, finish(): pl.pallas_call(finish_kernel, out_shape=(jax.ShapeDtypeStruct((TOK, D), b...  2.51 us

profile of v3, /device:TPU:1, one launch (start us, length us, event | category | flops | bytes accessed | tf_op | source)
XLA Modules:
  0.0 106.0 jit_solution(5967613027572646855)
XLA Ops:
  1.3 102.3 %step.1 = (bf16[96,1024]{1,0:T(8,128)(2,1)}, bf16[2,32,8,256]{3,2,1,0:T(8,128)(2,1)}, bf16[2,32,8,256]{3,2,1,0:T(8,128)(2,1)}, bf16[2,5,8,128]{3,2,1,0:T(8,128)(2,1)}) custom-call(bf16[96,128]{1,0:T(8,128)(2,1)} %pix.1, bf16[128,1024]{1,0:T(8,128)(2,1)} %bitcast.10, bf16[8,1024]{1,0:T(8,128)(2,1)} %bias.1, bf16[1,1024]{1,0:T(2,128)(2,1)} %aggq.1, ...), custom_call_target="tpu_custom_call" | custom-call | tf_op jit(solution)/shard_map/step/pallas_call | solution.py:553
  103.5 2.5 %finish.1 = (bf16[96,1024]{1,0:T(8,128)(2,1)}, f32[128,1024]{1,0:T(8,128)}, f32[8,1024]{1,0:T(8,128)}, f32[1,1024]{1,0:T(1,128)}, f32[64,1024]{1,0:T(8,128)}, /*...) custom-call(bf16[96,1024]{1,0:T(8,128)(2,1)} %get-tuple-element.20.layer_in, ...), custom_call_target="tpu_custom_call" | custom-call | tf_op jit(solution)/shard_map/finish/pallas_call | solution.py:648

commit v4 on v3

v4 whole, which is shorter than its diff:
```python
import jax
import jax.numpy as jnp
from jax import lax
from jax.experimental import pallas as pl
from jax.experimental.pallas import tpu as pltpu
from jax.sharding import PartitionSpec as P

MESH = pl.DeviceIdType.MESH
NX, NH, NY, NL = 4, 3, 8, 4
CH = NX * NH
TOK, D = 96, 1024
HEADS, HD = 12, 64
WIDE = HEADS * HD
CHANNELS, PP = 8, 16
PARTS = 3
PR = TOK // PARTS
PH = PR // 2
CAP = 15.0
OWN = NY * NL
FEW = 5
ROWS = CH * PR

f32, bf16 = jnp.float32, jnp.bfloat16


def dot(a, b, ca, cb):
    return lax.dot_general(a, b, (((ca,), (cb,)), ((), ())), preferred_element_type=f32)


def iota(shape, dim):
    return lax.broadcasted_iota(jnp.int32, shape, dim)


def split(value):
    high = value.astype(bf16)
    return high, (value - high.astype(f32)).astype(bf16)


def stacked(row):
    at = iota((8, 128), 0)
    out = jnp.zeros((8, 128), f32)
    for j in range(8):
        out = jnp.where(at == j, row[:, 128 * j : 128 * j + 128], out)
    return out


def step_kernel(
    pix_h,
    wemb_h,
    bias_h,
    aggq,
    kw_h,
    vw_h,
    fq,
    outw_h,
    counts,
    go_h,
    layer_h,
    out_a,
    out_b,
    out_c,
    layer,
    pix,
    wemb,
    bias,
    kw,
    vw,
    outw,
    go,
    emb,
    tok_all,
    w_all,
    kt_all,
    tok,
    wp,
    kt,
    head_o,
    kq,
    left,
    th_s,
    hp_s,
    pg_s,
    att_s,
    wide_s,
    g_a,
    g_b,
    g_c,
    half_a,
    half_b,
    half_c,
    held_a,
    held_b,
    held_c,
    mine_a,
    mine_b,
    mine_c,
    acc_a,
    acc_b,
    acc_c,
    sz,
    rz,
    sx,
    rx,
    sw,
    rw,
    sy,
    ry,
    sb,
    rb,
    s0,
    r0,
    s1,
    r1,
    r2,
    s3,
    r3,
    s4,
    s5,
):
    dp, ch = lax.axis_index("dp"), lax.axis_index("chan")
    x, zh = ch // NH, ch % NH
    core, own = dp % 2, dp // 2
    y, zl = own % NY, own // NY
    xn, xp = (x + 1) % NX, (x + NX - 1) % NX
    yn, yp = (y + 1) % NY, (y + NY - 1) % NY

    def at_chan(x_, z_):
        return (dp, x_ * NH + z_)

    def at_dp(y_, c_):
        return (zl * (2 * NY) + y_ * 2 + c_, ch)

    zdev = [at_chan(x, (zh + k + 1) % NH) for k in range(2)]
    xdev = [at_chan(xn, zh), at_chan(xp, zh)]
    ydev = [at_dp(yn, core), at_dp(yp, core)]
    sib = at_dp(y, 1 - core)

    loads = [
        pltpu.make_async_copy(src, dst, s5.at[i])
        for i, (src, dst) in enumerate(
            (
                (vw_h, vw),
                (outw_h, outw),
                (kw_h, kw),
                (pix_h, pix),
                (wemb_h, wemb),
                (bias_h, bias),
                (go_h, go),
            )
        )
    ]
    for copy in loads:
        copy.start()
    barrier = pltpu.get_barrier_semaphore()
    for dev in zdev + xdev + [sib]:
        pl.semaphore_signal(barrier, inc=1, device_id=dev, device_id_type=MESH)

    @pl.loop(1, OWN)
    def _(j):
        pl.semaphore_signal(
            barrier, inc=1, device_id=(((own + j) % OWN) * 2 + core, ch), device_id_type=MESH
        )

    for copy in loads[:3]:
        copy.wait()
    for q in range(4):
        wp[q] = vw[16 * q : 16 * q + 16, :]
        wp[4 + q] = outw[16 * q : 16 * q + 16, :]
    fq8 = jnp.broadcast_to(fq[...].astype(f32), (16, HD)).astype(bf16)
    kt[...] = stacked(dot(fq8, kw[...], 1, 0)[:1])
    kt_all[ch] = kt[...]
    kq[256 : 256 + HD] = vw[...]
    kq[256 + HD :] = jnp.zeros((HD, D), bf16)
    head_o[:HD] = outw[...]
    head_o[HD:] = jnp.zeros((HD, D), bf16)

    started = []

    def remote(src, dst, ss, rs, dev):
        return pltpu.make_async_remote_copy(
            src_ref=src, dst_ref=dst, send_sem=ss, recv_sem=rs, device_id=dev, device_id_type=MESH
        )

    def send(src, dst, ss, rs, dev):
        copy = remote(src, dst, ss, rs, dev)
        copy.start()
        started.append(copy)

    def arrive(dst, ss, rs):
        remote(dst, dst, ss, rs, sib).wait_recv()

    def owner(dx, k):
        return ((x + NX - dx) % NX) * NH + (zh + NH - k) % NH

    def at_rows(c, p, start, rows):
        return tok_all.at[pl.ds(pl.multiple_of(p * ROWS + c * PR + start, 16), rows)]

    lanes = pl.multiple_of(core * 512, 512)
    wmine = wp.at[y, :, pl.ds(lanes, 512)]

    def piece(c):
        at = y * CH + (c % NH) * NX + c // NH
        return w_all.at[pl.ds(pl.multiple_of(at * 16, 16), 16), pl.ds(lanes, 512)]

    small = [(wmine, piece), (kt, lambda c: kt_all.at[c])]

    def part(c, p):
        return at_rows(c, p, 0, PR)

    def half(c, p, h):
        return at_rows(c, p, h * PH, PH)

    pl.semaphore_wait(barrier, OWN + 4)
    place = pltpu.make_async_copy(wmine, piece(ch), s4)
    place.start()

    for i, (src, dst) in enumerate(small):
        for k in range(2):
            send(src, dst(ch), sw.at[i, k], rw.at[i, k], zdev[k])
        for d in range(2):
            send(src, dst(ch), sw.at[i, 2 + 3 * d], rw.at[i, 2 + 3 * d], xdev[d])
    for copy in loads[3:]:
        copy.wait()
    lane = iota((TOK, 128), 1)
    pixels = pix[...]
    query = aggq[...].astype(f32)
    score = jnp.zeros((TOK, 128), f32)
    for c in range(CHANNELS):
        masked = jnp.where((lane >= PP * c) & (lane < PP * (c + 1)), pixels, jnp.zeros_like(pixels))
        e = (dot(masked, wemb[...], 1, 0) + bias[c : c + 1, :].astype(f32)).astype(bf16)
        emb[c] = e
        s = jnp.sum(e.astype(f32) * query, 1, keepdims=True)
        score = jnp.where(lane == c, s, score)
    capped = CAP * jnp.tanh(score / CAP)
    agg_exp = jnp.exp(capped) * jnp.where(lane < counts[...], 1.0, 0.0)
    agg_weight = agg_exp / jnp.sum(agg_exp, 1, keepdims=True)
    agg_round = agg_weight.astype(bf16).astype(f32)
    token = jnp.zeros((TOK, D), f32)
    for c in range(CHANNELS):
        token += agg_round[:, c : c + 1] * emb[c].astype(f32)
    tok[...] = token.astype(bf16)
    for p in range(PARTS):
        tok_all[pl.ds(pl.multiple_of(p * ROWS + ch * PR, 32), PR), :] = tok[p * PR : p * PR + PR, :]

    for p in range(PARTS):
        own_part = tok.at[pl.ds(p * PR, PR)]
        for k in range(2):
            send(own_part, part(ch, p), sz.at[k, p], rz.at[k, p], zdev[k])
        for d in range(2):
            send(own_part, part(ch, p), sx.at[d, 0, p], rx.at[d, 0, p], xdev[d])

    place.wait()

    def relay(k, p):
        c = owner(1, k)
        arrive(part(c, p), sx.at[0, k, p], rx.at[0, k, p])
        send(half(c, p, 0), half(c, p, 0), sx.at[2, k, p], rx.at[2, k, p], xdev[0])
        c = owner(NX - 1, k)
        arrive(part(c, p), sx.at[1, k, p], rx.at[1, k, p])
        send(half(c, p, 1), half(c, p, 1), sx.at[3, k, p], rx.at[3, k, p], xdev[1])

    def small_relay(k):
        for i, (_, dst) in enumerate(small):
            c = owner(1, k)
            arrive(dst(c), sw.at[i, 2 + k], rw.at[i, 2 + k])
            send(dst(c), dst(c), sw.at[i, 8 + k], rw.at[i, 8 + k], xdev[0])

    def small_last(k):
        for i, (_, dst) in enumerate(small):
            c = owner(NX - 1, k)
            arrive(dst(c), sw.at[i, 5 + k], rw.at[i, 5 + k])
            c = owner(2, k)
            arrive(dst(c), sw.at[i, 8 + k], rw.at[i, 8 + k])

    def rows_of(y_, k, core_):
        at = ((y_ + 2 * NY) % NY) * (CH * 16) + ((zh + NH - k) % NH) * (NX * 16)
        return w_all.at[
            pl.ds(pl.multiple_of(at, 64), NX * 16), pl.ds(pl.multiple_of(core_ * 512, 512), 512)
        ]

    def sub(y_, k):
        return rows_of(y_, k, core)

    def goes(s, k, d):
        return s < 3 or (s == 3 and k % 2 == d)

    def ysend(s, k, d):
        block = sub(y - s, k) if d == 0 else sub(y + s, k)
        send(block, block, sy.at[d, s, k], ry.at[d, s, k], ydev[d])

    def ystart(k):
        for d in range(2):
            ysend(0, k, d)
        send(sub(y, k), sub(y, k), sb.at[2, 0, k], rb.at[2, 0, k], sib)

    def yarrive(s):
        for k in range(3):
            for d in range(2):
                if goes(s, k, d):
                    block = sub(y - 1 - s, k) if d == 0 else sub(y + 1 + s, k)
                    arrive(block, sy.at[d, s, k], ry.at[d, s, k])
                    if goes(s + 1, k, d):
                        ysend(s + 1, k, d)
                    send(block, block, sb.at[d, s, k], rb.at[d, s, k], sib)

    small_relay(0)
    for k in (1, 2):
        for i, (_, dst) in enumerate(small):
            c = owner(0, k)
            arrive(dst(c), sw.at[i, k - 1], rw.at[i, k - 1])
            for d in range(2):
                send(dst(c), dst(c), sw.at[i, 2 + 3 * d + k], rw.at[i, 2 + 3 * d + k], xdev[d])
    small_last(0)
    ystart(0)
    for p in range(PARTS):
        relay(0, p)
    for k in (1, 2):
        small_relay(k)
    for k in (1, 2):
        small_last(k)
        ystart(k)

    def load_scores():
        at = iota((128, 128), 0)
        for j in range(8):
            rows = jnp.zeros((128, 128), f32)
            for h in range(HEADS):
                rows = jnp.where(at == h, kt_all[h, j : j + 1, :], rows)
            high, low = split(rows)
            kq[:128, 128 * j : 128 * j + 128] = high
            kq[128:256, 128 * j : 128 * j + 128] = low

    lane_rows = iota((ROWS, 128), 1)
    mine_only = lane_rows == ch

    def folded(value):
        return jnp.sum(value.reshape(CH, PR, value.shape[1]), 0)

    def tiled(value):
        return jnp.concatenate([value] * CH, 0)

    def weight_of(hp):
        return jnp.sum(jnp.where(mine_only, hp.astype(bf16).astype(f32), 0.0), 1, keepdims=True)

    def part_scores(p):
        at, rows = slice(p * ROWS, p * ROWS + ROWS), slice(p * PR, p * PR + PR)
        for k in range(3):
            c = owner(2, k)
            arrive(half(c, p, 0), sx.at[2, k, p], rx.at[2, k, p])
            arrive(half(c, p, 1), sx.at[3, k, p], rx.at[3, k, p])
        r = dot(tok_all[at, :], kq[...], 1, 1)
        th = jnp.tanh((r[:, :128] + r[:, 128:256]) / 8.0 / CAP)
        ex = jnp.exp(CAP * th)
        hp = ex * tiled(1.0 / folded(ex))
        th_s[at, :] = th
        hp_s[at, :] = hp
        att_s[rows, :] = folded(weight_of(hp) * r[:, 256:].astype(bf16).astype(f32))

    for p in range(PARTS):
        for k in (1, 2):
            c = owner(0, k)
            arrive(part(c, p), sz.at[k - 1, p], rz.at[k - 1, p])
            for d in range(2):
                send(part(c, p), part(c, p), sx.at[d, k, p], rx.at[d, k, p], xdev[d])
        yarrive(p)
        if p == PARTS - 1:
            load_scores()
            part_scores(0)
        for k in (1, 2):
            relay(k, p)
    yarrive(3)
    for p in range(1, PARTS):
        part_scores(p)

    def put(ref, i, rows):
        for c in range(2):
            for q in range(2):
                at = 512 * c + 256 * q
                ref[c, 2 * i + q] = rows[:, at : at + 256].astype(bf16)

    def put_small(i, row):
        g_c[i // FEW, i % FEW] = stacked(row).astype(bf16)

    grads = go[...]
    of_grads = dot(att_s[...].astype(bf16), grads, 0, 0)
    for i in range(8):
        put(g_a, 8 + i, of_grads[8 * i : 8 * i + 8])
    my_grad = dot(grads, head_o[...], 1, 1).astype(bf16).astype(f32)

    for k in range(3):
        arrive(rows_of(y, k, 1 - core), sb.at[2, 0, k], rb.at[2, 0, k])
        for s in range(4):
            for d in range(2):
                if goes(s, k, d):
                    y_ = y - 1 - s if d == 0 else y + 1 + s
                    arrive(rows_of(y_, k, 1 - core), sb.at[d, s, k], rb.at[d, s, k])
    for copy in started:
        copy.wait_send()

    def fold(at):
        return at - 192 * sum((at >= 192 * n).astype(jnp.int32) for n in (1, 2, 3))

    def place_of(head):
        return 16 * (4 * head - 11 * sum((head >= 3 * n).astype(jnp.int32) for n in (1, 2, 3)))

    col, row = fold(iota((128, WIDE), 1)), place_of(iota((128, WIDE), 0))
    expand = jnp.where((col >= row) & (col < row + 16), 1.0, 0.0).astype(bf16)
    row, col = fold(iota((WIDE, 128), 0)), place_of(iota((WIDE, 128), 1))
    gather = jnp.where((row >= col) & (row < col + 16), 1.0, 0.0).astype(bf16)

    all_grad = dot(grads, w_all[WIDE:, :], 1, 1).astype(bf16).astype(f32)

    for p in range(PARTS):
        at, rows = slice(p * ROWS, p * ROWS + ROWS), slice(p * PR, p * PR + PR)
        v = dot(tok_all[at, :], w_all[:WIDE, :], 1, 1).astype(bf16).astype(f32)
        high, low = split(v * tiled(all_grad[rows]))
        prob_grad = dot(high, gather, 1, 0) + dot(low, gather, 1, 0)
        hp, th = hp_s[at, :], th_s[at, :]
        wide_s[rows, :] = folded(dot(hp.astype(bf16), expand, 1, 0) * v).astype(bf16)
        raw = hp * (prob_grad - tiled(folded(hp * prob_grad))) * (1.0 - th * th) / 8.0
        pg_s[at, :] = raw
        high, low = split(jnp.sum(jnp.where(mine_only, raw, 0.0), 1, keepdims=True))
        weighted = weight_of(hp) * tiled(my_grad[rows])
        weighted = jnp.where(lane_rows == HD, high.astype(f32), weighted)
        weighted = jnp.where(lane_rows == HD + 1, low.astype(f32), weighted)
        left[at, :] = weighted.astype(bf16)

    of_tokens = dot(left[...], tok_all[...], 0, 0)
    put_small(9, of_tokens[HD : HD + 1] + of_tokens[HD + 1 : HD + 2])
    for i in range(8):
        put(g_a, i, of_tokens[8 * i : 8 * i + 8])

    def pair(ref, half, n):
        return remote(ref.at[1 - core], half, s0.at[n], r0.at[n], sib)

    pair(g_a, half_a, 0).start()

    here = [pl.ds(pl.multiple_of(p * ROWS + ch * PR, 32), PR) for p in range(PARTS)]
    hp = jnp.concatenate([hp_s[at, :] for at in here], 0)
    raw = jnp.concatenate([pg_s[at, :] for at in here], 0)
    wide = dot(hp.astype(bf16), expand, 1, 0)
    high, low = split(raw)
    token_grad = (
        dot((wide * all_grad).astype(bf16), w_all[:WIDE, :], 1, 0)
        + dot(high, kq[:128], 1, 0)
        + dot(high, kq[128:256], 1, 0)
        + dot(low, kq[:128], 1, 0)
    )
    mix = jnp.zeros((TOK, 128), f32)
    for c in range(CHANNELS):
        s = jnp.sum(token_grad * emb[c].astype(f32), 1, keepdims=True)
        mix = jnp.where(lane == c, s, mix)
    agg_raw = (
        agg_weight
        * (mix - jnp.sum(agg_weight * mix, 1, keepdims=True))
        * (1.0 - (capped / CAP) * (capped / CAP))
    )

    def pair_sum(ref, half, acc, n):
        pair(ref, half, n).wait_recv()
        acc[...] = (ref[core].astype(f32) + half[...].astype(f32)).astype(bf16)

    def peer(j):
        return (j * 2 + core, ch)

    def spread_out(acc, held, n):
        @pl.loop(1, OWN)
        def _(j):
            to = (own + j) % OWN
            remote(acc.at[to], held.at[own], s1.at[n, to], r1.at[n, own], peer(to)).start()

    def total_of(acc, held, at, n):
        def add(j, total):
            src = (own + OWN - j) % OWN
            remote(held.at[src], held.at[src], s1.at[n, src], r1.at[n, src], sib).wait_recv()
            return total + held[src].astype(f32)

        return lax.fori_loop(1, OWN, add, acc[at].astype(f32)).astype(bf16)

    def give(mine, out, n):
        @pl.loop(1, OWN)
        def _(j):
            to = (own + j) % OWN
            remote(mine, out.at[core, own], s1.at[n, to], r2.at[n, own], peer(to)).start()

        out[core, own] = mine[...]

    pair_sum(g_a, half_a, acc_a, 0)
    spread_out(acc_a, held_a, 0)

    layer[...] = dot(wide_s[...], w_all[WIDE:, :], 1, 0).astype(bf16)
    store = pltpu.make_async_copy(layer, layer_h, s5.at[7])
    eye = (iota((128, 128), 0) == iota((128, 128), 1)).astype(f32).astype(bf16)
    upright = dot(eye, pixels, 1, 1)
    one = jnp.where(iota((16, TOK), 0) == 0, 1.0, 0.0)
    grad_agg = jnp.zeros((TOK, D), f32)
    for c in range(CHANNELS):
        e = (agg_round[:, c : c + 1] * token_grad + agg_raw[:, c : c + 1] * query).astype(bf16)
        grad_agg += agg_raw[:, c : c + 1] * emb[c].astype(f32)
        rows = jnp.concatenate([upright[PP * c : PP * c + PP], one], 0).astype(bf16)
        res = dot(rows, e, 1, 0)
        put_small(c, res[16:17])
        put(g_b, 2 * c, res[:8])
        put(g_b, 2 * c + 1, res[8:16])
    pair(g_b, half_b, 1).start()
    store.start()
    put_small(8, jnp.sum(grad_agg, 0, keepdims=True))

    pair_sum(g_b, half_b, acc_b, 1)
    pair(g_c, half_c, 2).start()
    spread_out(acc_b, held_b, 1)
    pair_sum(g_c, half_c, acc_c, 2)
    for i in range(FEW):

        @pl.when(own != i)
        def _():
            remote(acc_c.at[i], held_c.at[own], s1.at[2, i], r1.at[2, own], peer(i)).start()

    def spread_sent(acc, held, n):
        @pl.loop(1, OWN)
        def _(j):
            to = (own + j) % OWN
            remote(acc.at[to], held.at[own], s1.at[n, to], r1.at[n, own], sib).wait_send()

    mine_a[...] = total_of(acc_a, held_a, own, 0)
    spread_sent(acc_a, held_a, 0)
    give(mine_a, out_a, 0)
    mine_b[...] = total_of(acc_b, held_b, own, 1)
    spread_sent(acc_b, held_b, 1)
    give(mine_b, out_b, 1)
    for i in range(FEW):

        @pl.when(own != i)
        def _():
            remote(acc_c.at[i], held_c.at[own], s1.at[2, i], r1.at[2, own], sib).wait_send()

    @pl.when(own < FEW)
    def _():
        mine_c[...] = total_of(acc_c, held_c, own, 2)
        give(mine_c, out_c, 2)

    def taken(out, n):
        @pl.loop(1, OWN)
        def _(j):
            src = (own + OWN - j) % OWN
            block = out.at[core, src]
            remote(block, block, s1.at[n, src], r2.at[n, src], sib).wait_recv()

    def back(out, n):
        return remote(out.at[core], out.at[core], s3.at[n], r3.at[n], sib)

    taken(out_a, 0)
    back(out_a, 0).start()
    taken(out_b, 1)
    back(out_b, 1).start()
    for i in range(FEW):

        @pl.when(own != i)
        def _():
            block = out_c.at[core, i]
            remote(block, block, s1.at[2, i], r2.at[2, i], sib).wait_recv()

    back(out_c, 2).start()
    for n, out in enumerate((out_a, out_b, out_c)):
        other = out.at[1 - core]
        remote(other, other, s3.at[n], r3.at[n], sib).wait_recv()
        back(out, n).wait_send()
    for n, (ref, half) in enumerate(((g_a, half_a), (g_b, half_b), (g_c, half_c))):
        pair(ref, half, n).wait_send()

    def given(mine, out, n):
        @pl.loop(1, OWN)
        def _(j):
            to = (own + j) % OWN
            remote(mine, out.at[core, own], s1.at[n, to], r2.at[n, own], sib).wait_send()

    store.wait()
    given(mine_a, out_a, 0)
    given(mine_b, out_b, 1)

    @pl.when(own < FEW)
    def _():
        given(mine_c, out_c, 2)


def step(*args):
    vmem = pl.BlockSpec(memory_space=pltpu.VMEM)
    any_ = pl.BlockSpec(memory_space=pl.ANY)
    dma = pltpu.SemaphoreType.DMA
    large, few = (OWN, 8, 256), (FEW, 8, 128)
    return pl.pallas_call(
        step_kernel,
        out_shape=(
            jax.ShapeDtypeStruct((TOK, D), bf16),
            jax.ShapeDtypeStruct((2, *large), bf16),
            jax.ShapeDtypeStruct((2, *large), bf16),
            jax.ShapeDtypeStruct((2, *few), bf16),
        ),
        in_specs=[any_, any_, any_, vmem, any_, any_, vmem, any_, vmem, any_],
        out_specs=(any_, vmem, vmem, vmem),
        scratch_shapes=[
            pltpu.VMEM((TOK, D), bf16),
            pltpu.VMEM((TOK, CHANNELS * PP), bf16),
            pltpu.VMEM((CHANNELS * PP, D), bf16),
            pltpu.VMEM((CHANNELS, D), bf16),
            pltpu.VMEM((HD, D), bf16),
            pltpu.VMEM((HD, D), bf16),
            pltpu.VMEM((HD, D), bf16),
            pltpu.VMEM((TOK, D), bf16),
            pltpu.VMEM((CHANNELS, TOK, D), bf16),
            pltpu.VMEM((CH * TOK, D), bf16),
            pltpu.VMEM((NY * CH * 16, D), bf16),
            pltpu.VMEM((CH, 8, 128), f32),
            pltpu.VMEM((TOK, D), bf16),
            pltpu.VMEM((NY, 16, D), bf16),
            pltpu.VMEM((8, 128), f32),
            pltpu.VMEM((128, D), bf16),
            pltpu.VMEM((384, D), bf16),
            pltpu.VMEM((CH * TOK, 128), bf16),
            pltpu.VMEM((CH * TOK, 128), f32),
            pltpu.VMEM((CH * TOK, 128), f32),
            pltpu.VMEM((CH * TOK, 128), f32),
            pltpu.VMEM((TOK, 128), f32),
            pltpu.VMEM((TOK, WIDE), bf16),
            pltpu.VMEM((2, *large), bf16),
            pltpu.VMEM((2, *large), bf16),
            pltpu.VMEM((2, *few), bf16),
            pltpu.VMEM(large, bf16),
            pltpu.VMEM(large, bf16),
            pltpu.VMEM(few, bf16),
            pltpu.VMEM(large, bf16),
            pltpu.VMEM(large, bf16),
            pltpu.VMEM((OWN, 8, 128), bf16),
            pltpu.VMEM(large[1:], bf16),
            pltpu.VMEM(large[1:], bf16),
            pltpu.VMEM(few[1:], bf16),
            pltpu.VMEM(large, bf16),
            pltpu.VMEM(large, bf16),
            pltpu.VMEM(few, bf16),
            dma((2, PARTS)),
            dma((2, PARTS)),
            dma((4, 3, PARTS)),
            dma((4, 3, PARTS)),
            dma((2, 11)),
            dma((2, 11)),
            dma((2, 4, 3)),
            dma((2, 4, 3)),
            dma((3, 4, 3)),
            dma((3, 4, 3)),
            dma((3,)),
            dma((3,)),
            dma((3, OWN)),
            dma((3, OWN)),
            dma((3, OWN)),
            dma((3,)),
            dma((3,)),
            dma,
            dma((8,)),
        ],
        compiler_params=pltpu.CompilerParams(collective_id=0, has_side_effects=True),
        name="step",
    )(*args)


def finish_kernel(layer_in, a, b, few, fq, kw, layer, embed, bias, agg, key, value, query, outg):
    def rows(ref, i):
        parts = [ref[c, 2 * i + q] for c in range(2) for q in range(2)]
        return jnp.concatenate(parts, 1).astype(f32)

    def row(i):
        block = few[i // FEW, i % FEW].astype(f32)
        return jnp.concatenate([block[j : j + 1] for j in range(8)], 1)

    layer[...] = layer_in[...]
    for i in range(16):
        embed[8 * i : 8 * i + 8, :] = rows(b, i)
    for i in range(8):
        bias[i : i + 1, :] = row(i)
        value[8 * i : 8 * i + 8, :] = rows(a, i)
        outg[8 * i : 8 * i + 8, :] = rows(a, 8 + i)
    agg[...] = row(8)
    u_rows = jnp.broadcast_to(row(9), (16, D)).astype(bf16)
    only = jnp.where(iota((16, HD), 0) == 0, fq[...].astype(f32), 0.0).astype(bf16)
    key[...] = dot(only, u_rows, 0, 0)
    query[...] = dot(u_rows, kw[...], 1, 1)[:1]


def finish(*args):
    vmem = pl.BlockSpec(memory_space=pltpu.VMEM)

    def shape(*dims):
        return jax.ShapeDtypeStruct(dims, f32)

    return pl.pallas_call(
        finish_kernel,
        out_shape=(
            jax.ShapeDtypeStruct((TOK, D), bf16),
            shape(CHANNELS * PP, D),
            shape(CHANNELS, D),
            shape(1, D),
            shape(HD, D),
            shape(HD, D),
            shape(1, HD),
            shape(HD, D),
        ),
        in_specs=[vmem] * len(args),
        out_specs=(vmem,) * 8,
        name="finish",
    )(*args)


def per_device(
    pixels,
    embed_weight,
    channel_bias,
    agg_query,
    key_weight,
    value_weight,
    final_query,
    out_weight,
    group_counts,
    grad_output,
):
    key_rows = key_weight.T
    partial = step(
        pixels,
        embed_weight.reshape(CHANNELS * PP, D),
        channel_bias,
        agg_query,
        key_rows,
        value_weight.T,
        final_query,
        out_weight,
        group_counts.reshape(1, 1),
        grad_output,
    )
    layer_out, embed, bias, agg, key, value, query, outg = finish(*partial, final_query, key_rows)
    return layer_out, embed.reshape(CHANNELS, PP, D), bias, agg, key.T, value.T, query, outg


def solution(mesh):
    in_specs = (
        P("dp", "chan"),
        P("chan", None, None),
        P("chan", None),
        P("chan", None),
        P(None, "chan"),
        P(None, "chan"),
        P("chan", None),
        P("chan", None),
        P("chan"),
        P("dp", None),
    )
    out_specs = (
        P("dp", None),
        P("chan", None, None),
        P("chan", None),
        P("chan", None),
        P(None, "chan"),
        P(None, "chan"),
        P("chan", None),
        P("chan", None),
    )
    return jax.shard_map(
        per_device, mesh=mesh, in_specs=in_specs, out_specs=out_specs, check_vma=False
    )
```

time: 106 us -> 93.4 us (0.88)
  Pallas kernels: 105 us -> 91.9 us
    pallas_call x1, Pallas kernels: 102 us -> 89.4 us  [step(): pl.pallas_call(step_kernel, out_shape=(jax.ShapeDtypeStruct((TOK, D), bf1...]
where the time goes in v4:
time: 93.4 us; the launch traced here: 93.2 us
  Pallas kernels  91.9 us (98%)
  between operations  1.29 us (1%)
    pallas_call x1, Pallas kernels, step(): pl.pallas_call(step_kernel, out_shape=(jax.ShapeDtypeStruct((TOK, D), bf1...  89.4 us
    pallas_call x1, Pallas kernels, finish(): pl.pallas_call(finish_kernel, out_shape=(jax.ShapeDtypeStruct((TOK, D), b...  2.51 us

profile of v4, /device:TPU:1, one launch (start us, length us, event | category | flops | bytes accessed | tf_op | source)
XLA Modules:
  0.0 93.2 jit_solution(15187577661669563955)
XLA Ops:
  1.3 89.4 %step.1 = (bf16[96,1024]{1,0:T(8,128)(2,1)}, bf16[2,32,8,256]{3,2,1,0:T(8,128)(2,1)}, bf16[2,32,8,256]{3,2,1,0:T(8,128)(2,1)}, bf16[2,5,8,128]{3,2,1,0:T(8,128)(2,1)}) custom-call(bf16[96,128]{1,0:T(8,128)(2,1)} %pix_h.1, bf16[128,1024]{1,0:T(8,128)(2,1)} %bitcast.10, bf16[8,1024]{1,0:T(8,128)(2,1)} %bias_h.1, bf16[1,1024]{1,0:T(2,128)(2,1)} %aggq.1, ...), custom_call_target="tpu_custom_call" | custom-call | tf_op jit(solution)/shard_map/step/pallas_call | solution.py:591
  90.7 2.5 %finish.1 = (bf16[96,1024]{1,0:T(8,128)(2,1)}, f32[128,1024]{1,0:T(8,128)}, f32[8,1024]{1,0:T(8,128)}, f32[1,1024]{1,0:T(1,128)}, f32[64,1024]{1,0:T(8,128)}, /*...) custom-call(bf16[96,1024]{1,0:T(8,128)(2,1)} %get-tuple-element.20.layer_in, ...), custom_call_target="tpu_custom_call" | custom-call | tf_op jit(solution)/shard_map/finish/pallas_call | solution.py:694
